TPU v7x, 32 devices: a whole 2x2x4 slice. The times are simulated.
32 devices in a mesh: groups: 2 (over x), tm: 16 (over z, y, core).
Axes of the slice: x: 2, y: 2, z: 4, core: 2. Of those that a mesh axis runs over, the one named last changes fastest.
Arguments:
- queries: bfloat16 [12288, 2240], P(('groups', 'tm')), parts along dimension 0, may hold values from -40 to 40
- keys: bfloat16 [12288, 2240], P(('groups', 'tm')), parts along dimension 0, may hold values from -6 to 6
- values: bfloat16 [12288, 2240], P(('groups', 'tm')), parts along dimension 0, may hold values from -6 to 6
- cross_queries: bfloat16 [12288, 2240], P(('groups', 'tm')), parts along dimension 0, may hold values from -540 to 540
- prompt_keys: bfloat16 [32, 128, 2240], P(('groups', 'tm')), parts along dimension 0, may hold values from -6 to 6
- prompt_values: bfloat16 [32, 128, 2240], P(('groups', 'tm')), parts along dimension 0, may hold values from -6 to 6
- caption_keys: bfloat16 [256, 2240], P('groups'), parts along dimension 0, may hold values from -6 to 6
- caption_values: bfloat16 [256, 2240], P('groups'), parts along dimension 0, may hold values from -6 to 6
- span_start: int32 [32], P('groups'), parts along dimension 0, may hold values from 0 to 15, as said below
- span_end: int32 [32], P('groups'), parts along dimension 0, may hold values from 1 to 16
- prompt_tokens: int32 [32], P('groups'), parts along dimension 0, may hold values from 80 to 128, as said below
- region_mask: int32 [32, 3], P('groups'), parts along dimension 0, may hold values 0 or 1
- out_gain: float32 [2240], replicated, may hold values from 0.5 to 1.5
Outputs:
- self_mixed: bfloat16 [12288, 2240], P(('groups', 'tm')), parts along dimension 0
- cross_mixed: bfloat16 [12288, 2240], P(('groups', 'tm')), parts along dimension 0
There are 2 independent parts, one for each index of `groups`. A program takes and returns all parts, laid end to end along the dimension named above; an argument that names none is the same for every part. Nothing has to cross between parts.
Inputs may be any that keep to these rules, and one draw needn't show every extreme that they name: Prompt p applies to stretches span_start[p] to span_end[p] - 1, with p <= span_start[p] <= p + 1 and span_start[p] < span_end[p] <= p + 6; prompt 0 covers stretches 0 to 5. `prompt_tokens`: prompt 0 uses all 128 slots.
All inputs are finite; a program needn't handle non-finite values.
Results may differ from a plain program's by a relative error of at most 0.007.
Values may be sent and summed in bfloat16 or wider, within the bound.
A program may use at most 128 MiB of HBM per device.

v0:
```python
import math

import jax
import jax.numpy as jnp
from jax import lax
from jax.sharding import PartitionSpec as P

HD = 32
SPAN = 6
PR_DEV = 1
PL = 128


def prefix(value, axis, join, neutral):
    place = lax.axis_index(axis)
    gathered = lax.all_gather(value.astype(jnp.bfloat16), axis)
    state = jnp.zeros_like(value) + jnp.asarray(neutral, value.dtype)

    def one(hop, state):
        return join(state, lax.dynamic_index_in_dim(gathered, hop, 0, False).astype(value.dtype))

    return lax.fori_loop(0, place, one, state)


def passed_along(block, axis, distance):
    devices = range(lax.axis_size(axis))
    route = [(i - distance, i) for i in devices if i - distance in devices]
    return lax.ppermute(block, axis, route)


def add_states(earlier, later):
    return earlier + later


def prompt_tiles(owner_id, stretch_id, span_start, span_end, prompt_tokens, region_mask):
    first_row = jnp.maximum(owner_id, 0) * PR_DEV
    begins = lax.dynamic_slice_in_dim(span_start, first_row, PR_DEV, 0)
    finish = lax.dynamic_slice_in_dim(span_end, first_row, PR_DEV, 0)
    counts = lax.dynamic_slice_in_dim(prompt_tokens, first_row, PR_DEV, 0)
    regions = lax.dynamic_slice_in_dim(region_mask, first_row, PR_DEV, 0)
    covers = (owner_id >= 0) & (begins <= stretch_id) & (stretch_id < finish)
    live_keys = jnp.arange(PL, dtype=jnp.int32)[None, :] < counts[:, None]
    visible_set = covers[:, None, None] & (regions[:, :, None] == 1) & live_keys[:, None, :]
    return jnp.transpose(visible_set, (1, 0, 2)).reshape(regions.shape[1], PR_DEV * PL)


def per_token(tile_mask, tok_rows):
    tile_count, key_count = tile_mask.shape
    spread_out = jnp.broadcast_to(
        tile_mask[:, None, :], (tile_count, tok_rows // tile_count, key_count)
    )
    return spread_out.reshape(tok_rows, key_count)


def attend_block(state_in, query_rows, block_keys, block_values, visible):
    run_max, run_sum, running = state_in
    tok_rows, head_count, head_size = query_rows.shape
    keys_three = block_keys.reshape(block_keys.shape[0], head_count, head_size)
    values_three = block_values.reshape(block_values.shape[0], head_count, head_size)
    scores = jnp.einsum(
        "rhd,khd->hrk", query_rows, keys_three, preferred_element_type=jnp.float32
    ) * head_size ** (-0.5)
    scores = jnp.where(visible[None], scores, -1e30)
    new_max = jnp.maximum(run_max, jnp.max(scores, axis=2))
    expo = jnp.where(visible[None], jnp.exp(scores - new_max[:, :, None]), 0.0)
    run_sum = jnp.sum(expo, axis=2)
    added = jnp.einsum(
        "hrk,khd->rhd", expo.astype(jnp.bfloat16), values_three, preferred_element_type=jnp.float32
    )
    running = added
    return (new_max, run_sum, running)


def empty_state(head_count, tok_rows):
    return (
        jnp.full((head_count, tok_rows), -1e30, jnp.float32),
        jnp.zeros((head_count, tok_rows), jnp.float32),
        jnp.zeros((tok_rows, head_count, HD), jnp.float32),
    )


def joined_attention(query_rows, all_keys, all_values, visible):
    tok_rows, head_count, head_size = query_rows.shape
    key_count = all_keys.shape[0]
    group = math.gcd(head_count, 10)
    group_count = head_count // group
    query_groups = jnp.transpose(
        query_rows.reshape(tok_rows, group_count, group, head_size), (1, 0, 2, 3)
    )
    key_groups = jnp.transpose(
        all_keys.reshape(key_count, group_count, group * head_size), (1, 0, 2)
    )
    value_groups = jnp.transpose(
        all_values.reshape(key_count, group_count, group * head_size), (1, 0, 2)
    )

    def one_group(packed):
        query_part, key_part, value_part = packed
        run_max, run_sum, running = attend_block(
            empty_state(group, tok_rows), query_part, key_part, value_part, visible
        )
        return running / jnp.transpose(run_sum)[:, :, None]

    mixed_groups = lax.map(one_group, (query_groups, key_groups, value_groups))
    return jnp.transpose(mixed_groups, (1, 0, 2, 3)).reshape(tok_rows, head_count * head_size)


def local(
    queries,
    keys,
    values,
    cross_queries,
    prompt_keys,
    prompt_values,
    caption_keys,
    caption_values,
    span_start,
    span_end,
    prompt_tokens,
    region_mask,
    out_gain,
):
    tok_rows, model_width = queries.shape
    head_count = model_width // HD
    stretch_id = lax.axis_index("tm")
    lifted_keys = jnp.maximum(keys, 0).reshape(tok_rows, head_count, HD)
    stretch_state = jnp.einsum(
        "rhd,rhe->hde",
        lifted_keys,
        values.reshape(tok_rows, head_count, HD),
        preferred_element_type=jnp.float32,
    )
    prior_state = prefix(
        stretch_state.reshape(head_count, HD * HD),
        "tm",
        add_states,
        jnp.zeros((head_count, HD * HD), jnp.float32),
    )
    whole_state = (prior_state.reshape(head_count, HD, HD) + stretch_state).astype(jnp.bfloat16)
    lifted_queries = jnp.maximum(queries, 0).reshape(tok_rows, head_count, HD)
    raw_mix = jnp.einsum(
        "rhd,hde->rhe", lifted_queries, whole_state, preferred_element_type=jnp.float32
    ).reshape(tok_rows, model_width)
    mean_square = jnp.mean(raw_mix * raw_mix, axis=-1, keepdims=True)
    self_mixed = (raw_mix * lax.rsqrt(mean_square + 1e-05) * out_gain[None, :]).astype(jnp.bfloat16)
    query_rows = cross_queries.reshape(tok_rows, head_count, HD)
    caption_seen = jnp.ones((tok_rows, caption_keys.shape[0]), dtype=bool)
    slot_count = prompt_keys.shape[0] * prompt_keys.shape[1]
    blocks = [(prompt_keys, prompt_values)]
    moving = (prompt_keys, prompt_values)
    for reach in range(1, SPAN):
        moving = passed_along((moving[0], moving[1]), "tm", 1)
        blocks.append(moving)
    block_keys = [blocks[reach][0].reshape(slot_count, model_width) for reach in range(SPAN)]
    block_values = [blocks[reach][1].reshape(slot_count, model_width) for reach in range(SPAN)]
    block_seen = [
        per_token(
            prompt_tiles(
                stretch_id - reach, stretch_id, span_start, span_end, prompt_tokens, region_mask
            ),
            tok_rows,
        )
        for reach in range(SPAN)
    ]
    all_keys = jnp.concatenate([caption_keys] + block_keys, axis=0)
    all_values = jnp.concatenate([caption_values] + block_values, axis=0)
    visible = jnp.concatenate([caption_seen] + block_seen, axis=1)
    cross_mixed = joined_attention(query_rows, all_keys, all_values, visible).astype(jnp.bfloat16)
    return (self_mixed, cross_mixed)


def solution(mesh):
    in_specs = (
        P(("groups", "tm"), None),
        P(("groups", "tm"), None),
        P(("groups", "tm"), None),
        P(("groups", "tm"), None),
        P(("groups", "tm"), None, None),
        P(("groups", "tm"), None, None),
        P("groups", None),
        P("groups", None),
        P("groups"),
        P("groups"),
        P("groups"),
        P("groups", None),
        P(),
    )
    out_specs = (P(("groups", "tm"), None), P(("groups", "tm"), None))
    return jax.shard_map(local, mesh=mesh, in_specs=in_specs, out_specs=out_specs, check_vma=False)
```

profile of v0, /device:TPU:24, one launch (start us, length us, event | category | flops | bytes accessed | tf_op | source)
XLA Modules:
  0.0 229.2 jit_solution(11526491504432644969)
XLA Ops:
  7.2 2.1 collective-permute-start
  9.3 3.5 %collective-permute-start.5 = (bf16[1,128,2240]{1,2,0:T(8,128)(2,1)}, bf16[1,128,2240]{1,2,0:T(8,128)(2,1)}, u32[]{:S(2)}, u32[]{:S(2)}) collective-permute-start(bf16[1,128,2240]{1,2,0:T(8,128)(2,1)} %param.21), channel_id=1, source_target_pairs={{0,1},{1,2},{2,3},{3,4},{4,5},{5,6},{6,7},{7,8},{8,9},{9,10},{10,1... | collective-permute-start | bytes 1720328 | tf_op jit(solution)/shard_map/ppermute | solution.py:28
  31.0 2.0 constant_dynamic-update-slice_fusion.6
  32.9 2.0 constant_dynamic-update-slice_fusion.19
  34.9 1.9 constant_dynamic-update-slice_fusion.5
  37.8 1.9 collective-permute-start.1
  39.7 1.9 collective-permute-start.6
  43.0 13.1 %collective-permute-done.1 = bf16[1,128,2240]{1,2,0:T(8,128)(2,1)} collective-permute-done((bf16[1,128,2240]{1,2,0:T(8,128)(2,1)}, bf16[1,128,2240]{1,2,0:T(8,128)(2,1)}, u32[]{:S(2)}, u32[]{:S(2)}) %collective-permute-start.1) | collective-permute-done | bytes 573472 | tf_op jit(solution)/shard_map/ppermute | solution.py:28
  56.1 1.9 collective-permute-start.2
  58.6 7.1 %collective-permute-done.6 = bf16[1,128,2240]{1,2,0:T(8,128)(2,1)} collective-permute-done((bf16[1,128,2240]{1,2,0:T(8,128)(2,1)}, bf16[1,128,2240]{1,2,0:T(8,128)(2,1)}, u32[]{:S(2)}, u32[]{:S(2)}) %collective-permute-start.6) | collective-permute-done | bytes 573472 | tf_op jit(solution)/shard_map/ppermute | solution.py:28
  65.6 1.9 collective-permute-start.7
  70.0 1.8 collective-permute-done.2
  71.8 1.9 collective-permute-start.3
  73.8 4.2 %collective-permute-done.7 = bf16[1,128,2240]{1,2,0:T(8,128)(2,1)} collective-permute-done((bf16[1,128,2240]{1,2,0:T(8,128)(2,1)}, bf16[1,128,2240]{1,2,0:T(8,128)(2,1)}, u32[]{:S(2)}, u32[]{:S(2)}) %collective-permute-start.7) | collective-permute-done | bytes 573472 | tf_op jit(solution)/shard_map/ppermute | solution.py:28
  77.9 1.9 collective-permute-start.8
  79.9 1.9 constant_dynamic-update-slice_fusion.4
  81.8 2.0 constant_dynamic-update-slice_fusion.17
  83.8 2.0 constant_dynamic-update-slice_fusion.3
  85.8 1.9 collective-permute-start.4
  87.7 2.0 constant_dynamic-update-slice_fusion.16
  90.1 1.9 collective-permute-start.9
  92.0 2.0 constant_dynamic-update-slice_fusion.2
  94.0 1.9 constant_dynamic-update-slice_fusion.15
  98.7 5.1 %collective-permute-done.9 = bf16[1,128,2240]{1,2,0:T(8,128)(2,1)S(1)} collective-permute-done((bf16[1,128,2240]{1,2,0:T(8,128)(2,1)S(1)}, bf16[1,128,2240]{1,2,0:T(8,128)(2,1)S(1)}, u32[]{:S(2)}, u32[]{:S(2)}) %collective-permute-start.9) | collective-permute-done | bytes 573472 | tf_op jit(solution)/shard_map/ppermute | solution.py:28
  104.7 100.3 %while.21 = (s32[]{:T(128)}, bf16[7,384,10,32]{1,3,2,0:T(8,128)(2,1)}, bf16[7,896,320]{1,2,0:T(8,128)(2,1)}, pred[384,896]{1,0:T(8,128)(4,1)S(1)}, bf16[7,384,10...) while((s32[]{:T(128)}, bf16[7,384,10,32]{1,3,2,0:T(8,128)(2,1)}, ...), condition=%wide.region_6.7_spmd, body=%wide.region_3.6_spmd.sunk | while | flops 485249280 | bytes 46606416 | solution.py:104
  106.1 3.8 %fusion.59 = (f32[10,384]{1,0:T(8,128)S(1)}, f32[10,384,896]{2,1,0:T(8,128)S(1)}) fusion(pred[384,896]{1,0:T(8,128)(4,1)S(1)} %get-tuple-element.230, bf16[896,10,32]{0,2,1:T(8,128)(2,1)S(1)} %bitcast.111, bf16[7,384,10,32]{1,3,2,0:T(8,128)(2,1)} %get-tuple-element.231, s32[]{:T(128)} %get-tuple-element.220), kind=kOutput, calls=%fused_computation.3.clone.1 | convolution fusion | flops 230519040 | bytes 14941696 | tf_op jit(solution)/shard_map/while/body/eval_jaxpr/rhd,khd->hrk/dot_general | solution.py:60
  109.9 4.3 %fusion.60 = f32[10,384]{1,0:T(8,128)S(1)} fusion(f32[10,384,896]{2,1,0:T(8,128)S(1)} %get-tuple-element.190, f32[10,384]{1,0:T(8,128)S(1)} %broadcast_maximum_fusion.4, pred[384,896]{1,0:T(8,128)(4,1)S(1)} %get-tuple-element.230), kind=kLoop, calls=%fused_computation.4.clone.1 | loop fusion | flops 17199360 | bytes 14137344 | tf_op jit(solution)/shard_map/while/body/eval_jaxpr/reduce_sum | solution.py:66
  114.2 4.9 %fusion.61 = bf16[7,384,10,32]{1,3,2,0:T(8,128)(2,1)} fusion(bf16[7,384,10,32]{1,3,2,0:T(8,128)(2,1)} %get-tuple-element.221, s32[]{:T(128)} %get-tuple-element.220, bf16[896,10,32]{0,2,1:T(8,128)(2,1)S(1)} %bitcast.112, f32[10,384,896]{2,1,0:T(8,128)S(1)} %get-tuple-element.190, f32[10,384]{1,0:T(8,128)S(1)} %broadcast_maximum_fusion.4, ...), kind=kOutput, calls=%fused_computation.11.clone.1 | convolution fusion | flops 237527040 | bytes 15202816 | tf_op jit(solution)/shard_map/while/body/eval_jaxpr/hrk,khd->rhd/dot_general | solution.py:67
  120.4 3.8 %fusion.59 = (f32[10,384]{1,0:T(8,128)S(1)}, f32[10,384,896]{2,1,0:T(8,128)S(1)}) fusion(pred[384,896]{1,0:T(8,128)(4,1)S(1)} %get-tuple-element.230, bf16[896,10,32]{0,2,1:T(8,128)(2,1)S(1)} %bitcast.111, bf16[7,384,10,32]{1,3,2,0:T(8,128)(2,1)} %get-tuple-element.231, s32[]{:T(128)} %get-tuple-element.220), kind=kOutput, calls=%fused_computation.3.clone.1 | convolution fusion | flops 230519040 | bytes 14941696 | tf_op jit(solution)/shard_map/while/body/eval_jaxpr/rhd,khd->hrk/dot_general | solution.py:60
  124.2 4.3 %fusion.60 = f32[10,384]{1,0:T(8,128)S(1)} fusion(f32[10,384,896]{2,1,0:T(8,128)S(1)} %get-tuple-element.190, f32[10,384]{1,0:T(8,128)S(1)} %broadcast_maximum_fusion.4, pred[384,896]{1,0:T(8,128)(4,1)S(1)} %get-tuple-element.230), kind=kLoop, calls=%fused_computation.4.clone.1 | loop fusion | flops 17199360 | bytes 14137344 | tf_op jit(solution)/shard_map/while/body/eval_jaxpr/reduce_sum | solution.py:66
  128.5 4.9 %fusion.61 = bf16[7,384,10,32]{1,3,2,0:T(8,128)(2,1)} fusion(bf16[7,384,10,32]{1,3,2,0:T(8,128)(2,1)} %get-tuple-element.221, s32[]{:T(128)} %get-tuple-element.220, bf16[896,10,32]{0,2,1:T(8,128)(2,1)S(1)} %bitcast.112, f32[10,384,896]{2,1,0:T(8,128)S(1)} %get-tuple-element.190, f32[10,384]{1,0:T(8,128)S(1)} %broadcast_maximum_fusion.4, ...), kind=kOutput, calls=%fused_computation.11.clone.1 | convolution fusion | flops 237527040 | bytes 15202816 | tf_op jit(solution)/shard_map/while/body/eval_jaxpr/hrk,khd->rhd/dot_general | solution.py:67
  134.7 3.8 %fusion.59 = (f32[10,384]{1,0:T(8,128)S(1)}, f32[10,384,896]{2,1,0:T(8,128)S(1)}) fusion(pred[384,896]{1,0:T(8,128)(4,1)S(1)} %get-tuple-element.230, bf16[896,10,32]{0,2,1:T(8,128)(2,1)S(1)} %bitcast.111, bf16[7,384,10,32]{1,3,2,0:T(8,128)(2,1)} %get-tuple-element.231, s32[]{:T(128)} %get-tuple-element.220), kind=kOutput, calls=%fused_computation.3.clone.1 | convolution fusion | flops 230519040 | bytes 14941696 | tf_op jit(solution)/shard_map/while/body/eval_jaxpr/rhd,khd->hrk/dot_general | solution.py:60
  138.5 4.3 %fusion.60 = f32[10,384]{1,0:T(8,128)S(1)} fusion(f32[10,384,896]{2,1,0:T(8,128)S(1)} %get-tuple-element.190, f32[10,384]{1,0:T(8,128)S(1)} %broadcast_maximum_fusion.4, pred[384,896]{1,0:T(8,128)(4,1)S(1)} %get-tuple-element.230), kind=kLoop, calls=%fused_computation.4.clone.1 | loop fusion | flops 17199360 | bytes 14137344 | tf_op jit(solution)/shard_map/while/body/eval_jaxpr/reduce_sum | solution.py:66
  142.8 4.9 %fusion.61 = bf16[7,384,10,32]{1,3,2,0:T(8,128)(2,1)} fusion(bf16[7,384,10,32]{1,3,2,0:T(8,128)(2,1)} %get-tuple-element.221, s32[]{:T(128)} %get-tuple-element.220, bf16[896,10,32]{0,2,1:T(8,128)(2,1)S(1)} %bitcast.112, f32[10,384,896]{2,1,0:T(8,128)S(1)} %get-tuple-element.190, f32[10,384]{1,0:T(8,128)S(1)} %broadcast_maximum_fusion.4, ...), kind=kOutput, calls=%fused_computation.11.clone.1 | convolution fusion | flops 237527040 | bytes 15202816 | tf_op jit(solution)/shard_map/while/body/eval_jaxpr/hrk,khd->rhd/dot_general | solution.py:67
  149.1 3.8 %fusion.59 = (f32[10,384]{1,0:T(8,128)S(1)}, f32[10,384,896]{2,1,0:T(8,128)S(1)}) fusion(pred[384,896]{1,0:T(8,128)(4,1)S(1)} %get-tuple-element.230, bf16[896,10,32]{0,2,1:T(8,128)(2,1)S(1)} %bitcast.111, bf16[7,384,10,32]{1,3,2,0:T(8,128)(2,1)} %get-tuple-element.231, s32[]{:T(128)} %get-tuple-element.220), kind=kOutput, calls=%fused_computation.3.clone.1 | convolution fusion | flops 230519040 | bytes 14941696 | tf_op jit(solution)/shard_map/while/body/eval_jaxpr/rhd,khd->hrk/dot_general | solution.py:60
  152.9 4.3 %fusion.60 = f32[10,384]{1,0:T(8,128)S(1)} fusion(f32[10,384,896]{2,1,0:T(8,128)S(1)} %get-tuple-element.190, f32[10,384]{1,0:T(8,128)S(1)} %broadcast_maximum_fusion.4, pred[384,896]{1,0:T(8,128)(4,1)S(1)} %get-tuple-element.230), kind=kLoop, calls=%fused_computation.4.clone.1 | loop fusion | flops 17199360 | bytes 14137344 | tf_op jit(solution)/shard_map/while/body/eval_jaxpr/reduce_sum | solution.py:66
  157.2 4.9 %fusion.61 = bf16[7,384,10,32]{1,3,2,0:T(8,128)(2,1)} fusion(bf16[7,384,10,32]{1,3,2,0:T(8,128)(2,1)} %get-tuple-element.221, s32[]{:T(128)} %get-tuple-element.220, bf16[896,10,32]{0,2,1:T(8,128)(2,1)S(1)} %bitcast.112, f32[10,384,896]{2,1,0:T(8,128)S(1)} %get-tuple-element.190, f32[10,384]{1,0:T(8,128)S(1)} %broadcast_maximum_fusion.4, ...), kind=kOutput, calls=%fused_computation.11.clone.1 | convolution fusion | flops 237527040 | bytes 15202816 | tf_op jit(solution)/shard_map/while/body/eval_jaxpr/hrk,khd->rhd/dot_general | solution.py:67
  163.4 3.8 %fusion.59 = (f32[10,384]{1,0:T(8,128)S(1)}, f32[10,384,896]{2,1,0:T(8,128)S(1)}) fusion(pred[384,896]{1,0:T(8,128)(4,1)S(1)} %get-tuple-element.230, bf16[896,10,32]{0,2,1:T(8,128)(2,1)S(1)} %bitcast.111, bf16[7,384,10,32]{1,3,2,0:T(8,128)(2,1)} %get-tuple-element.231, s32[]{:T(128)} %get-tuple-element.220), kind=kOutput, calls=%fused_computation.3.clone.1 | convolution fusion | flops 230519040 | bytes 14941696 | tf_op jit(solution)/shard_map/while/body/eval_jaxpr/rhd,khd->hrk/dot_general | solution.py:60
  167.2 4.3 %fusion.60 = f32[10,384]{1,0:T(8,128)S(1)} fusion(f32[10,384,896]{2,1,0:T(8,128)S(1)} %get-tuple-element.190, f32[10,384]{1,0:T(8,128)S(1)} %broadcast_maximum_fusion.4, pred[384,896]{1,0:T(8,128)(4,1)S(1)} %get-tuple-element.230), kind=kLoop, calls=%fused_computation.4.clone.1 | loop fusion | flops 17199360 | bytes 14137344 | tf_op jit(solution)/shard_map/while/body/eval_jaxpr/reduce_sum | solution.py:66
  171.5 4.9 %fusion.61 = bf16[7,384,10,32]{1,3,2,0:T(8,128)(2,1)} fusion(bf16[7,384,10,32]{1,3,2,0:T(8,128)(2,1)} %get-tuple-element.221, s32[]{:T(128)} %get-tuple-element.220, bf16[896,10,32]{0,2,1:T(8,128)(2,1)S(1)} %bitcast.112, f32[10,384,896]{2,1,0:T(8,128)S(1)} %get-tuple-element.190, f32[10,384]{1,0:T(8,128)S(1)} %broadcast_maximum_fusion.4, ...), kind=kOutput, calls=%fused_computation.11.clone.1 | convolution fusion | flops 237527040 | bytes 15202816 | tf_op jit(solution)/shard_map/while/body/eval_jaxpr/hrk,khd->rhd/dot_general | solution.py:67
  177.7 3.8 %fusion.59 = (f32[10,384]{1,0:T(8,128)S(1)}, f32[10,384,896]{2,1,0:T(8,128)S(1)}) fusion(pred[384,896]{1,0:T(8,128)(4,1)S(1)} %get-tuple-element.230, bf16[896,10,32]{0,2,1:T(8,128)(2,1)S(1)} %bitcast.111, bf16[7,384,10,32]{1,3,2,0:T(8,128)(2,1)} %get-tuple-element.231, s32[]{:T(128)} %get-tuple-element.220), kind=kOutput, calls=%fused_computation.3.clone.1 | convolution fusion | flops 230519040 | bytes 14941696 | tf_op jit(solution)/shard_map/while/body/eval_jaxpr/rhd,khd->hrk/dot_general | solution.py:60
  181.5 4.3 %fusion.60 = f32[10,384]{1,0:T(8,128)S(1)} fusion(f32[10,384,896]{2,1,0:T(8,128)S(1)} %get-tuple-element.190, f32[10,384]{1,0:T(8,128)S(1)} %broadcast_maximum_fusion.4, pred[384,896]{1,0:T(8,128)(4,1)S(1)} %get-tuple-element.230), kind=kLoop, calls=%fused_computation.4.clone.1 | loop fusion | flops 17199360 | bytes 14137344 | tf_op jit(solution)/shard_map/while/body/eval_jaxpr/reduce_sum | solution.py:66
  185.8 4.9 %fusion.61 = bf16[7,384,10,32]{1,3,2,0:T(8,128)(2,1)} fusion(bf16[7,384,10,32]{1,3,2,0:T(8,128)(2,1)} %get-tuple-element.221, s32[]{:T(128)} %get-tuple-element.220, bf16[896,10,32]{0,2,1:T(8,128)(2,1)S(1)} %bitcast.112, f32[10,384,896]{2,1,0:T(8,128)S(1)} %get-tuple-element.190, f32[10,384]{1,0:T(8,128)S(1)} %broadcast_maximum_fusion.4, ...), kind=kOutput, calls=%fused_computation.11.clone.1 | convolution fusion | flops 237527040 | bytes 15202816 | tf_op jit(solution)/shard_map/while/body/eval_jaxpr/hrk,khd->rhd/dot_general | solution.py:67
  192.1 3.8 %fusion.59 = (f32[10,384]{1,0:T(8,128)S(1)}, f32[10,384,896]{2,1,0:T(8,128)S(1)}) fusion(pred[384,896]{1,0:T(8,128)(4,1)S(1)} %get-tuple-element.230, bf16[896,10,32]{0,2,1:T(8,128)(2,1)S(1)} %bitcast.111, bf16[7,384,10,32]{1,3,2,0:T(8,128)(2,1)} %get-tuple-element.231, s32[]{:T(128)} %get-tuple-element.220), kind=kOutput, calls=%fused_computation.3.clone.1 | convolution fusion | flops 230519040 | bytes 14941696 | tf_op jit(solution)/shard_map/while/body/eval_jaxpr/rhd,khd->hrk/dot_general | solution.py:60
  195.9 4.3 %fusion.60 = f32[10,384]{1,0:T(8,128)S(1)} fusion(f32[10,384,896]{2,1,0:T(8,128)S(1)} %get-tuple-element.190, f32[10,384]{1,0:T(8,128)S(1)} %broadcast_maximum_fusion.4, pred[384,896]{1,0:T(8,128)(4,1)S(1)} %get-tuple-element.230), kind=kLoop, calls=%fused_computation.4.clone.1 | loop fusion | flops 17199360 | bytes 14137344 | tf_op jit(solution)/shard_map/while/body/eval_jaxpr/reduce_sum | solution.py:66
  200.2 4.9 %fusion.61 = bf16[7,384,10,32]{1,3,2,0:T(8,128)(2,1)} fusion(bf16[7,384,10,32]{1,3,2,0:T(8,128)(2,1)} %get-tuple-element.221, s32[]{:T(128)} %get-tuple-element.220, bf16[896,10,32]{0,2,1:T(8,128)(2,1)S(1)} %bitcast.112, f32[10,384,896]{2,1,0:T(8,128)S(1)} %get-tuple-element.190, f32[10,384]{1,0:T(8,128)S(1)} %broadcast_maximum_fusion.4, ...), kind=kOutput, calls=%fused_computation.11.clone.1 | convolution fusion | flops 237527040 | bytes 15202816 | tf_op jit(solution)/shard_map/while/body/eval_jaxpr/hrk,khd->rhd/dot_general | solution.py:67
  205.1 12.2 %while.20 = (s32[]{:T(128)}, f32[70,1024]{1,0:T(8,128)S(1)}, s32[]{:T(128)}, bf16[16,70,1024]{2,1,0:T(8,128)(2,1)}, s32[]{:T(128)}, /*index=5*/s32[]{:T(128)}, s32[]{:T(128)}) while((s32[]{:T(128)}, f32[70,1024]{1,0:T(8,128)S(1)}, s32[]{:T(128)}, bf16[16,70,1024]{2,1,0:T(8,128)(2,1)}, s32[]{:T(128)}, /*index=5*/s32[]{:T(128)}, s32[]{:T(128)}) %tuple.70), condition=%wide.region_1.2_spmd, body=%wide.region_0.1_spmd.sunk | while | flops 143365 | bytes 716915 | solution.py:22
  218.6 2.1 fusion.27
  (98 shorter events, 44.0 us)
Async XLA Ops:
  7.2 7.3 %copy-start = (bf16[384,2240]{0,1:T(8,128)(2,1)S(1)}, bf16[384,2240]{0,1:T(8,128)(2,1)}, u32[]{:S(2)}) copy-start(bf16[384,2240]{0,1:T(8,128)(2,1)} %param.19) | copy-start | bytes 5160964
  7.2 197.9 %all-gather.2.cloned.1.call-start = ((), (), s32[]{:S(2)}) async-start(), calls=%async_computation | async-start | bytes 2506752 | tf_op jit(solution)/shard_map/all_gather | solution.py:16
  7.2 30.6 %collective-permute-start = (bf16[1,128,2240]{1,2,0:T(8,128)(2,1)}, bf16[1,128,2240]{1,2,0:T(8,128)(2,1)}, u32[]{:S(2)}, u32[]{:S(2)}) collective-permute-start(bf16[1,128,2240]{1,2,0:T(8,128)(2,1)} %param.22), channel_id=1, source_target_pairs={{0,1},{1,2},{2,3},{3,4},{4,5},{5,6},{6,7},{7,8},{8,9},{9,10},{10,1... | collective-permute-start | bytes 1720328 | tf_op jit(solution)/shard_map/ppermute | solution.py:28
  9.3 30.4 %collective-permute-start.5 = (bf16[1,128,2240]{1,2,0:T(8,128)(2,1)}, bf16[1,128,2240]{1,2,0:T(8,128)(2,1)}, u32[]{:S(2)}, u32[]{:S(2)}) collective-permute-start(bf16[1,128,2240]{1,2,0:T(8,128)(2,1)} %param.21), channel_id=1, source_target_pairs={{0,1},{1,2},{2,3},{3,4},{4,5},{5,6},{6,7},{7,8},{8,9},{9,10},{10,1... | collective-permute-start | bytes 1720328 | tf_op jit(solution)/shard_map/ppermute | solution.py:28
  14.4 4.2 %copy-start.5 = (s32[16]{0:T(128)S(1)}, s32[16]{0:T(128)}, u32[]{:S(2)}) copy-start(s32[16]{0:T(128)} %param.25) | copy-start | bytes 196
  14.5 5.6 %copy-start.6 = (s32[16]{0:T(128)S(1)}, s32[16]{0:T(128)}, u32[]{:S(2)}) copy-start(s32[16]{0:T(128)} %param.27) | copy-start | bytes 196
  14.5 5.6 %copy-start.7 = (s32[16]{0:T(128)S(1)}, s32[16]{0:T(128)}, u32[]{:S(2)}) copy-start(s32[16]{0:T(128)} %param.26) | copy-start | bytes 196
  14.5 15.7 %copy-start.4 = (s32[16,3]{0,1:T(4,128)S(1)}, s32[16,3]{0,1:T(4,128)}, u32[]{:S(2)}) copy-start(s32[16,3]{0,1:T(4,128)} %param.28) | copy-start | bytes 580
  18.6 18.2 %copy-start.3 = (bf16[1,128,2240]{1,2,0:T(8,128)(2,1)S(1)}, bf16[1,128,2240]{1,2,0:T(8,128)(2,1)}, u32[]{:S(2)}) copy-start(bf16[1,128,2240]{1,2,0:T(8,128)(2,1)} %param.21) | copy-start | bytes 1720324
  18.7 23.0 %copy-start.2 = (bf16[384,2240]{0,1:T(8,128)(2,1)S(1)}, bf16[384,2240]{0,1:T(8,128)(2,1)}, u32[]{:S(2)}) copy-start(bf16[384,2240]{0,1:T(8,128)(2,1)} %param.17) | copy-start | bytes 5160964
  37.8 18.3 %collective-permute-start.1 = (bf16[1,128,2240]{1,2,0:T(8,128)(2,1)}, bf16[1,128,2240]{1,2,0:T(8,128)(2,1)}, u32[]{:S(2)}, u32[]{:S(2)}) collective-permute-start(bf16[1,128,2240]{1,2,0:T(8,128)(2,1)} %collective-permute-done), channel_id=1, source_target_pairs={{0,1},{1,2},{2,3},{3,4},{4,5},{5,6},{6,7},{7,8},{8,9},{9,10},{10,1... | collective-permute-start | bytes 1720328 | tf_op jit(solution)/shard_map/ppermute | solution.py:28
  39.7 25.9 %collective-permute-start.6 = (bf16[1,128,2240]{1,2,0:T(8,128)(2,1)}, bf16[1,128,2240]{1,2,0:T(8,128)(2,1)}, u32[]{:S(2)}, u32[]{:S(2)}) collective-permute-start(bf16[1,128,2240]{1,2,0:T(8,128)(2,1)} %collective-permute-done.5), channel_id=1, source_target_pairs={{0,1},{1,2},{2,3},{3,4},{4,5},{5,6},{6,7},{7,8},{8,9},{9,10},{10,1... | collective-permute-start | bytes 1720328 | tf_op jit(solution)/shard_map/ppermute | solution.py:28
  56.1 15.7 %collective-permute-start.2 = (bf16[1,128,2240]{1,2,0:T(8,128)(2,1)}, bf16[1,128,2240]{1,2,0:T(8,128)(2,1)}, u32[]{:S(2)}, u32[]{:S(2)}) collective-permute-start(bf16[1,128,2240]{1,2,0:T(8,128)(2,1)} %collective-permute-done.1), channel_id=1, source_target_pairs={{0,1},{1,2},{2,3},{3,4},{4,5},{5,6},{6,7},{7,8},{8,9},{9,10},{10,1... | collective-permute-start | bytes 1720328 | tf_op jit(solution)/shard_map/ppermute | solution.py:28
  65.6 12.3 %collective-permute-start.7 = (bf16[1,128,2240]{1,2,0:T(8,128)(2,1)}, bf16[1,128,2240]{1,2,0:T(8,128)(2,1)}, u32[]{:S(2)}, u32[]{:S(2)}) collective-permute-start(bf16[1,128,2240]{1,2,0:T(8,128)(2,1)} %collective-permute-done.6), channel_id=1, source_target_pairs={{0,1},{1,2},{2,3},{3,4},{4,5},{5,6},{6,7},{7,8},{8,9},{9,10},{10,1... | collective-permute-start | bytes 1720328 | tf_op jit(solution)/shard_map/ppermute | solution.py:28
  71.8 14.0 %collective-permute-start.3 = (bf16[1,128,2240]{1,2,0:T(8,128)(2,1)}, bf16[1,128,2240]{1,2,0:T(8,128)(2,1)S(1)}, u32[]{:S(2)}, u32[]{:S(2)}) collective-permute-start(bf16[1,128,2240]{1,2,0:T(8,128)(2,1)} %collective-permute-done.2), channel_id=1, source_target_pairs={{0,1},{1,2},{2,3},{3,4},{4,5},{5,6},{6,7},{7,8},{8,9},{9,10},{10,1... | collective-permute-start | bytes 1720328 | tf_op jit(solution)/shard_map/ppermute | solution.py:28
  77.9 12.2 %collective-permute-start.8 = (bf16[1,128,2240]{1,2,0:T(8,128)(2,1)}, bf16[1,128,2240]{1,2,0:T(8,128)(2,1)S(1)}, u32[]{:S(2)}, u32[]{:S(2)}) collective-permute-start(bf16[1,128,2240]{1,2,0:T(8,128)(2,1)} %collective-permute-done.7), channel_id=1, source_target_pairs={{0,1},{1,2},{2,3},{3,4},{4,5},{5,6},{6,7},{7,8},{8,9},{9,10},{10,1... | collective-permute-start | bytes 1720328 | tf_op jit(solution)/shard_map/ppermute | solution.py:28
  85.8 12.0 %collective-permute-start.4 = (bf16[1,128,2240]{1,2,0:T(8,128)(2,1)S(1)}, bf16[1,128,2240]{1,2,0:T(8,128)(2,1)S(1)}, u32[]{:S(2)}, u32[]{:S(2)}) collective-permute-start(bf16[1,128,2240]{1,2,0:T(8,128)(2,1)S(1)} %collective-permute-done.3), channel_id=1, source_target_pairs={{0,1},{1,2},{2,3},{3,4},{4,5},{5,6},{6,7},{7,8},{8,9},{9,10},{10,1... | collective-permute-start | bytes 1720328 | tf_op jit(solution)/shard_map/ppermute | solution.py:28
  90.1 13.7 %collective-permute-start.9 = (bf16[1,128,2240]{1,2,0:T(8,128)(2,1)S(1)}, bf16[1,128,2240]{1,2,0:T(8,128)(2,1)S(1)}, u32[]{:S(2)}, u32[]{:S(2)}) collective-permute-start(bf16[1,128,2240]{1,2,0:T(8,128)(2,1)S(1)} %collective-permute-done.8), channel_id=1, source_target_pairs={{0,1},{1,2},{2,3},{3,4},{4,5},{5,6},{6,7},{7,8},{8,9},{9,10},{10,1... | collective-permute-start | bytes 1720328 | tf_op jit(solution)/shard_map/ppermute | solution.py:28
  205.1 12.4 %copy-start.1 = (f32[70,32,32]{0,2,1:T(8,128)S(1)}, f32[70,32,32]{0,2,1:T(8,128)}, u32[]{:S(2)}) copy-start(f32[70,32,32]{0,2,1:T(8,128)} %copy.29) | copy-start | bytes 860164
  217.5 3.2 %copy-start.8 = (f32[2240]{0:T(1024)S(1)}, f32[2240]{0:T(1024)}, u32[]{:S(2)}) copy-start(f32[2240]{0:T(1024)} %param.29) | copy-start | bytes 26884
Sparse Core Ops, SparseCore 0:
  18.7 44.0 all-gather.1
where the time goes:
time: 231 us; the launch traced here: 229 us
  matrix products  64.5 us (28%)
  other arithmetic  51 us (22%)
  local copies, waits for them, and re-layouts  38.6 us (17%)
  waiting for transfers between devices  31.8 us (14%)
  between operations  22 us (10%)
  starting transfers between devices  20.9 us (9%)
    dot_general x7, matrix products, attend_block(): jnp.einsum('hrk,khd->rhd', expo.astype(jnp.bfloat16), values_three, prefe...  34.4 us
    ppermute x10, waiting for transfers between devices, passed_along(): return lax.ppermute(block, axis, route)  31.7 us
    reduce_sum x7, other arithmetic, attend_block(): run_sum = jnp.sum(expo, axis=2)  30 us
    dot_general x7, matrix products, attend_block(): jnp.einsum('rhd,khd->hrk', query_rows, keys_three, preferred_element_type...  26.5 us
    ppermute x10, starting transfers between devices, passed_along(): return lax.ppermute(block, axis, route)  20.9 us
    unnamed x36, local copies, waits for them, and re-layouts  20.6 us
    add x12, other arithmetic, add_states(): return earlier + later  11.9 us
    dynamic_slice x7, local copies, waits for them, and re-layouts, joined_attention(): mixed_groups = lax.map(one_group, (query_groups, key_groups, value_groups))  9.27 us
  transfers between devices with their start and end apart: 11, of which 6 were waited for; matrix products, arithmetic and copies ran while one was open for 60% of the time, Pallas kernels for 0%

commit v1 on v0

v1 whole, which is shorter than its diff:
```python
import functools
import math

import jax
import jax.numpy as jnp
from jax import lax
from jax.experimental import pallas as pl
from jax.experimental.pallas import tpu as pltpu
from jax.sharding import PartitionSpec as P

HD = 32
SPAN = 6
LANES = 128
HEADS = LANES // HD
NEG = -1e30


def state_kernel(k_ref, v_ref, s_ref):
    lifted = jnp.maximum(k_ref[...], 0)
    full = lax.dot_general(
        lifted, v_ref[...], (((0,), (0,)), ((), ())), preferred_element_type=jnp.float32
    )
    lane_head = lax.broadcasted_iota(jnp.int32, (HD, LANES), 1) // HD
    total = jnp.zeros((HD, LANES), jnp.float32)
    for h in range(HEADS):
        total = jnp.where(lane_head == h, full[h * HD : (h + 1) * HD, :], total)
    s_ref[...] = total


def stretch_states(keys, values):
    rows, width = keys.shape
    steps = pl.cdiv(width, LANES)
    spec = pl.BlockSpec((rows, LANES), lambda g: (0, g))
    return pl.pallas_call(
        state_kernel,
        grid=(steps,),
        in_specs=[spec, spec],
        out_specs=pl.BlockSpec((HD, LANES), lambda g: (0, g)),
        out_shape=jax.ShapeDtypeStruct((HD, width), jnp.float32),
    )(keys, values)


def mix_kernel(width, q_ref, own_ref, prior_ref, gain_ref, o_ref, raw_ref):
    steps = pl.cdiv(width, LANES)
    rows = q_ref.shape[0]
    square = jnp.zeros((rows, LANES), jnp.float32)
    for g in range(steps):
        lanes = min(LANES, width - g * LANES)
        part = pl.ds(g * LANES, lanes)
        small = (own_ref[:, part] + prior_ref[:, part]).astype(jnp.bfloat16)
        tall = jnp.concatenate([small] * (lanes // HD), axis=0)
        row_head = lax.broadcasted_iota(jnp.int32, (lanes, lanes), 0) // HD
        lane_head = lax.broadcasted_iota(jnp.int32, (lanes, lanes), 1) // HD
        weights = jnp.where(row_head == lane_head, tall, jnp.zeros_like(tall))
        raw = jnp.dot(
            jnp.maximum(q_ref[:, part], 0), weights, preferred_element_type=jnp.float32
        )
        raw_ref[:, part] = raw
        if lanes == LANES:
            square = square + raw * raw
        else:
            tail = jnp.sum(raw * raw, axis=1, keepdims=True)
    total = jnp.sum(square, axis=1, keepdims=True)
    if width % LANES:
        total = total + tail
    scale = lax.rsqrt(total * (1.0 / width) + 1e-05)
    for g in range(steps):
        part = pl.ds(g * LANES, min(LANES, width - g * LANES))
        o_ref[:, part] = (raw_ref[:, part] * scale * gain_ref[:, part]).astype(o_ref.dtype)


def self_mix(queries, own, prior, gain):
    rows, width = queries.shape
    return pl.pallas_call(
        functools.partial(mix_kernel, width),
        out_shape=jax.ShapeDtypeStruct((rows, width), jnp.bfloat16),
        scratch_shapes=[pltpu.VMEM((rows, width), jnp.float32)],
        compiler_params=pltpu.CompilerParams(vmem_limit_bytes=48 * 1024 * 1024),
    )(queries, own, prior, gain[None, :])


def attend_kernel(
    width, slots, tile_rows, tiles, least,
    seen_ref, list_ref, count_ref,
    q_ref, ck_ref, cv_ref, pk_ref, pv_ref, o_ref, k_buf, v_buf,
):
    g = pl.program_id(0)
    live = width - g * LANES
    lane = lax.broadcasted_iota(jnp.int32, (slots, LANES), 1)
    inside = lane < live
    for b in range(SPAN + 1):
        key_block = ck_ref[...] if b == 0 else pk_ref[b - 1]
        value_block = cv_ref[...] if b == 0 else pv_ref[b - 1]
        k_buf[b] = jnp.where(inside, key_block, jnp.zeros_like(key_block))
        v_buf[b] = value_block.T
    tok_lane = lax.broadcasted_iota(jnp.int32, (tile_rows, LANES), 1) // HD
    factor = HD ** (-0.5) * math.log2(math.e)

    def tile(t, blocks):
        first = pl.multiple_of(t * tile_rows, tile_rows)
        q = q_ref[pl.ds(first, tile_rows), :]
        ids = [0] + [list_ref[t * SPAN + i] for i in range(blocks - 1)]
        counts = [None] + [count_ref[ids[i]] for i in range(1, blocks)]
        outs = []
        for pair in range(HEADS // 2):
            heads = (2 * pair, 2 * pair + 1)
            both = jnp.concatenate(
                [jnp.where(tok_lane == h, q, jnp.zeros_like(q)) for h in heads], axis=0
            )
            scores = []
            peak = None
            for i in range(blocks):
                s = lax.dot_general(
                    k_buf[ids[i]], both, (((1,), (1,)), ((), ())),
                    preferred_element_type=jnp.float32,
                )
                if i:
                    row = lax.broadcasted_iota(jnp.int32, (slots - least, 2 * tile_rows), 0) + least
                    s = jnp.concatenate(
                        [s[:least], jnp.where(row < counts[i], s[least:], NEG)], axis=0
                    )
                top = jnp.max(s.reshape(slots // 8, 8, 2 * tile_rows), axis=0)
                peak = top if peak is None else jnp.maximum(peak, top)
                scores.append(s)
            peak = jnp.max(peak, axis=0, keepdims=True)
            denom = None
            acc = None
            for i in range(blocks):
                e = jnp.exp2((scores[i] - peak) * factor)
                part = jnp.sum(e.reshape(slots // 8, 8, 2 * tile_rows), axis=0)
                denom = part if denom is None else denom + part
                added = jnp.dot(
                    v_buf[ids[i], pl.ds(pair * 2 * HD, 2 * HD), :], e.astype(jnp.bfloat16),
                    preferred_element_type=jnp.float32,
                )
                acc = added if acc is None else acc + added
            inverse = 1.0 / jnp.sum(denom, axis=0, keepdims=True)
            outs.append(acc[:HD, :tile_rows] * inverse[:, :tile_rows])
            outs.append(acc[HD:, tile_rows:] * inverse[:, tile_rows:])
        mixed = jnp.concatenate(outs, axis=0)
        o_ref[pl.ds(first, tile_rows), :] = mixed.T.astype(o_ref.dtype)

    @pl.loop(0, tiles)
    def _(t):
        for blocks in range(1, SPAN + 2):
            @pl.when(seen_ref[t] == blocks - 1)
            def _():
                tile(t, blocks)


def cross_mix(queries, caption_keys, caption_values, near_keys, near_values, seen, order, counts):
    rows, width = queries.shape
    slots = caption_keys.shape[0]
    tiles = seen.shape[0]
    steps = pl.cdiv(width, LANES)
    token = pl.BlockSpec((rows, LANES), lambda g, *_: (0, g))
    caption = pl.BlockSpec((slots, LANES), lambda g, *_: (0, g))
    near = pl.BlockSpec((SPAN, slots, LANES), lambda g, *_: (0, 0, g))
    return pl.pallas_call(
        functools.partial(attend_kernel, width, slots, rows // tiles, tiles, slots * 5 // 8),
        grid_spec=pltpu.PrefetchScalarGridSpec(
            num_scalar_prefetch=3,
            grid=(steps,),
            in_specs=[token, caption, caption, near, near],
            out_specs=token,
            scratch_shapes=[
                pltpu.VMEM((SPAN + 1, slots, LANES), jnp.bfloat16),
                pltpu.VMEM((SPAN + 1, LANES, slots), jnp.bfloat16),
            ],
        ),
        out_shape=jax.ShapeDtypeStruct((rows, width), jnp.bfloat16),
        compiler_params=pltpu.CompilerParams(vmem_limit_bytes=48 * 1024 * 1024),
    )(seen, order, counts, queries, caption_keys, caption_values, near_keys, near_values)


def tables(stretch, span_start, span_end, prompt_tokens, region_mask):
    reach = jnp.arange(SPAN, dtype=jnp.int32)
    owner = stretch - reach
    row = jnp.maximum(owner, 0)
    covers = (owner >= 0) & (span_start[row] <= stretch) & (stretch < span_end[row])
    flags = (covers[:, None] & (region_mask[row] == 1)).T.astype(jnp.int32)
    seen = jnp.sum(flags, axis=1)
    place = jnp.cumsum(flags, axis=1) - 1
    hit = (place[:, :, None] == reach[None, None, :]) & (flags[:, :, None] == 1)
    order = jnp.sum(jnp.where(hit, reach[None, :, None] + 1, 0), axis=1)
    counts = jnp.concatenate([jnp.zeros((1,), jnp.int32), prompt_tokens[row]])
    return seen, order.reshape(-1), counts


def local(
    queries, keys, values, cross_queries, prompt_keys, prompt_values, caption_keys,
    caption_values, span_start, span_end, prompt_tokens, region_mask, out_gain,
):
    stretch = lax.axis_index("tm")
    devices = lax.axis_size("tm")
    own = stretch_states(keys, values)
    gathered = lax.all_gather(own.astype(jnp.bfloat16), "tm")
    earlier = jnp.arange(devices) < stretch
    prior = jnp.sum(
        jnp.where(earlier[:, None, None], gathered.astype(jnp.float32), 0.0), axis=0
    )
    self_mixed = self_mix(queries, own, prior, out_gain)
    route = [(i - 1, i) for i in range(1, devices)]
    moving = (prompt_keys, prompt_values)
    blocks = [moving]
    for _ in range(1, SPAN):
        moving = lax.ppermute(moving, "tm", route)
        blocks.append(moving)
    near_keys = jnp.concatenate([b[0] for b in blocks], axis=0)
    near_values = jnp.concatenate([b[1] for b in blocks], axis=0)
    seen, order, counts = tables(stretch, span_start, span_end, prompt_tokens, region_mask)
    cross_mixed = cross_mix(
        cross_queries, caption_keys, caption_values, near_keys, near_values, seen, order, counts
    )
    return (self_mixed, cross_mixed)


def solution(mesh):
    rows = P(("groups", "tm"), None)
    blocks = P(("groups", "tm"), None, None)
    in_specs = (
        rows, rows, rows, rows, blocks, blocks, P("groups", None), P("groups", None),
        P("groups"), P("groups"), P("groups"), P("groups", None), P(),
    )
    return jax.shard_map(
        local, mesh=mesh, in_specs=in_specs, out_specs=(rows, rows), check_vma=False
    )
```

time: 231 us -> 211 us (0.913)
  the two profiles are of different devices: /device:TPU:24 before, /device:TPU:20 now
where the time goes in v1:
time: 211 us; the launch traced here: 208 us
  local copies, waits for them, and re-layouts  75.8 us (36%)
  Pallas kernels  70 us (33%)
  starting transfers between devices  30.8 us (15%)
  between operations  14.3 us (7%)
  waiting for transfers between devices  9.45 us (4%)
  other arithmetic  7.15 us (3%)
    pallas_call x1, Pallas kernels, cross_mix(): pl.pallas_call(functools.partial(attend_kernel, width, slots, rows // til...  57 us
    unnamed x55, local copies, waits for them, and re-layouts  46.1 us
    ppermute x10, starting transfers between devices, local(): moving = lax.ppermute(moving, 'tm', route)  30.8 us
    ppermute x10, local copies, waits for them, and re-layouts, local(): moving = lax.ppermute(moving, 'tm', route)  21.3 us
    pallas_call x1, Pallas kernels, stretch_states(): pl.pallas_call(state_kernel, grid=(steps,), in_specs=[spec, spec], out_sp...  11.9 us
    ppermute x10, waiting for transfers between devices, local(): moving = lax.ppermute(moving, 'tm', route)  9.43 us
  transfers between devices with their start and end apart: 11, of which 3 were waited for; matrix products, arithmetic and copies ran while one was open for 35% of the time, Pallas kernels for 33%

profile of v1, /device:TPU:20, one launch (start us, length us, event | category | flops | bytes accessed | tf_op | source)
XLA Modules:
  0.0 207.6 jit_solution(8105530729869189691)
XLA Ops:
  7.2 2.1 collective-permute-start
  9.3 3.5 %collective-permute-start.5 = (bf16[1,128,2240]{1,2,0:T(8,128)(2,1)}, bf16[1,128,2240]{1,2,0:T(8,128)(2,1)}, u32[]{:S(2)}, u32[]{:S(2)}) collective-permute-start(bf16[1,128,2240]{1,2,0:T(8,128)(2,1)} %param.18), channel_id=1, source_target_pairs={{0,1},{1,2},{2,3},{3,4},{4,5},{5,6},{6,7},{7,8},{8,9},{9,10},{10,1... | collective-permute-start | bytes 1720328 | tf_op jit(solution)/shard_map/ppermute | solution.py:207
  12.8 3.8 %copy.68.k_ref = bf16[384,2240]{1,0:T(8,128)(2,1)} copy(bf16[384,2240]{0,1:T(8,128)(2,1)} %param.14) | data formatting | bytes 3440640 | tf_op args[1]
  16.7 2.4 %copy.69.v_ref = bf16[384,2240]{1,0:T(8,128)(2,1)} copy(bf16[384,2240]{0,1:T(8,128)(2,1)S(1)} %copy-done.10) | data formatting | bytes 3440640 | tf_op args[2]
  19.0 11.9 %shard_map.140.own_ref = f32[32,2240]{1,0:T(8,128)} custom-call(bf16[384,2240]{1,0:T(8,128)(2,1)} %copy.68.k_ref, bf16[384,2240]{1,0:T(8,128)(2,1)} %copy.69.v_ref), custom_call_target="tpu_custom_call" | custom-call | tf_op jit(solution)/shard_map/pallas_call | solution.py:34
  31.0 1.6 convert_element_type.12
  38.5 1.1 gather_fusion.3
  39.6 2.6 %copy.86.q_ref = bf16[384,2240]{1,0:T(8,128)(2,1)S(1)} copy(bf16[384,2240]{0,1:T(8,128)(2,1)} %param.16) | data formatting | bytes 3440640 | tf_op args[3]
  44.4 2.6 %copy.70.q_ref = bf16[384,2240]{1,0:T(8,128)(2,1)S(1)} copy(bf16[384,2240]{0,1:T(8,128)(2,1)} %param.13) | data formatting | bytes 3440640 | tf_op args[0]
  48.3 1.2 pad_add_fusion.count_ref
  49.5 1.3 convert_reduce_fusion.seen_ref
  50.8 1.9 constant_dynamic-update-slice_fusion.11
  52.7 1.9 collective-permute-start.1
  54.7 2.1 %copy.75 = bf16[1,128,2240]{2,1,0:T(8,128)(2,1)} copy(bf16[1,128,2240]{1,2,0:T(8,128)(2,1)} %collective-permute-done) | data formatting | bytes 1146880 | tf_op jit(solution)/shard_map/ppermute | solution.py:207
  56.8 3.5 %collective-permute-start.6 = (bf16[1,128,2240]{1,2,0:T(8,128)(2,1)}, bf16[1,128,2240]{1,2,0:T(8,128)(2,1)}, u32[]{:S(2)}, u32[]{:S(2)}) collective-permute-start(bf16[1,128,2240]{1,2,0:T(8,128)(2,1)} %collective-permute-done.5), channel_id=1, source_target_pairs={{0,1},{1,2},{2,3},{3,4},{4,5},{5,6},{6,7},{7,8},{8,9},{9,10},{10,1... | collective-permute-start | bytes 1720328 | tf_op jit(solution)/shard_map/ppermute | solution.py:207
  60.4 2.1 %copy.81 = bf16[1,128,2240]{2,1,0:T(8,128)(2,1)} copy(bf16[1,128,2240]{1,2,0:T(8,128)(2,1)} %collective-permute-done.5) | data formatting | bytes 1146880 | tf_op jit(solution)/shard_map/ppermute | solution.py:207
  62.5 1.9 constant_dynamic-update-slice_fusion.4
  64.4 1.9 constant_dynamic-update-slice_fusion.10
  66.3 4.1 %collective-permute-done.1 = bf16[1,128,2240]{1,2,0:T(8,128)(2,1)} collective-permute-done((bf16[1,128,2240]{1,2,0:T(8,128)(2,1)}, bf16[1,128,2240]{1,2,0:T(8,128)(2,1)}, u32[]{:S(2)}, u32[]{:S(2)}) %collective-permute-start.1) | collective-permute-done | bytes 573472 | tf_op jit(solution)/shard_map/ppermute | solution.py:207
  70.4 2.1 %copy.76 = bf16[1,128,2240]{2,1,0:T(8,128)(2,1)} copy(bf16[1,128,2240]{1,2,0:T(8,128)(2,1)} %collective-permute-done.1) | data formatting | bytes 1146880 | tf_op jit(solution)/shard_map/ppermute | solution.py:207
  72.5 1.9 collective-permute-start.2
  74.4 2.1 %collective-permute-done.6 = bf16[1,128,2240]{1,2,0:T(8,128)(2,1)} collective-permute-done((bf16[1,128,2240]{1,2,0:T(8,128)(2,1)}, bf16[1,128,2240]{1,2,0:T(8,128)(2,1)}, u32[]{:S(2)}, u32[]{:S(2)}) %collective-permute-start.6) | collective-permute-done | bytes 573472 | tf_op jit(solution)/shard_map/ppermute | solution.py:207
  76.5 2.1 %copy.82 = bf16[1,128,2240]{2,1,0:T(8,128)(2,1)} copy(bf16[1,128,2240]{1,2,0:T(8,128)(2,1)} %collective-permute-done.6) | data formatting | bytes 1146880 | tf_op jit(solution)/shard_map/ppermute | solution.py:207
  78.7 4.2 %collective-permute-start.7 = (bf16[1,128,2240]{1,2,0:T(8,128)(2,1)}, bf16[1,128,2240]{1,2,0:T(8,128)(2,1)}, u32[]{:S(2)}, u32[]{:S(2)}) collective-permute-start(bf16[1,128,2240]{1,2,0:T(8,128)(2,1)} %collective-permute-done.6), channel_id=1, source_target_pairs={{0,1},{1,2},{2,3},{3,4},{4,5},{5,6},{6,7},{7,8},{8,9},{9,10},{10,1... | collective-permute-start | bytes 1720328 | tf_op jit(solution)/shard_map/ppermute | solution.py:207
  82.9 1.9 constant_dynamic-update-slice_fusion.3
  84.8 1.9 constant_dynamic-update-slice_fusion.9
  86.8 2.1 %copy.77 = bf16[1,128,2240]{2,1,0:T(8,128)(2,1)} copy(bf16[1,128,2240]{1,2,0:T(8,128)(2,1)} %collective-permute-done.2) | data formatting | bytes 1146880 | tf_op jit(solution)/shard_map/ppermute | solution.py:207
  88.9 5.3 %collective-permute-start.3 = (bf16[1,128,2240]{1,2,0:T(8,128)(2,1)}, bf16[1,128,2240]{1,2,0:T(8,128)(2,1)}, u32[]{:S(2)}, u32[]{:S(2)}) collective-permute-start(bf16[1,128,2240]{1,2,0:T(8,128)(2,1)} %collective-permute-done.2), channel_id=1, source_target_pairs={{0,1},{1,2},{2,3},{3,4},{4,5},{5,6},{6,7},{7,8},{8,9},{9,10},{10,1... | collective-permute-start | bytes 1720328 | tf_op jit(solution)/shard_map/ppermute | solution.py:207
  94.2 2.1 %copy.83 = bf16[1,128,2240]{2,1,0:T(8,128)(2,1)} copy(bf16[1,128,2240]{1,2,0:T(8,128)(2,1)} %collective-permute-done.7) | data formatting | bytes 1146880 | tf_op jit(solution)/shard_map/ppermute | solution.py:207
  96.3 1.9 collective-permute-start.8
  98.2 1.9 constant_dynamic-update-slice_fusion.2
  100.2 1.9 constant_dynamic-update-slice_fusion.8
  102.1 2.1 %copy.78 = bf16[1,128,2240]{2,1,0:T(8,128)(2,1)} copy(bf16[1,128,2240]{1,2,0:T(8,128)(2,1)} %collective-permute-done.3) | data formatting | bytes 1146880 | tf_op jit(solution)/shard_map/ppermute | solution.py:207
  104.2 4.3 %collective-permute-start.4 = (bf16[1,128,2240]{1,2,0:T(8,128)(2,1)}, bf16[1,128,2240]{1,2,0:T(8,128)(2,1)}, u32[]{:S(2)}, u32[]{:S(2)}) collective-permute-start(bf16[1,128,2240]{1,2,0:T(8,128)(2,1)} %collective-permute-done.3), channel_id=1, source_target_pairs={{0,1},{1,2},{2,3},{3,4},{4,5},{5,6},{6,7},{7,8},{8,9},{9,10},{10,1... | collective-permute-start | bytes 1720328 | tf_op jit(solution)/shard_map/ppermute | solution.py:207
  108.5 2.1 %copy.84 = bf16[1,128,2240]{2,1,0:T(8,128)(2,1)} copy(bf16[1,128,2240]{1,2,0:T(8,128)(2,1)} %collective-permute-done.8) | data formatting | bytes 1146880 | tf_op jit(solution)/shard_map/ppermute | solution.py:207
  110.7 2.1 %collective-permute-start.9 = (bf16[1,128,2240]{1,2,0:T(8,128)(2,1)}, bf16[1,128,2240]{1,2,0:T(8,128)(2,1)}, u32[]{:S(2)}, u32[]{:S(2)}) collective-permute-start(bf16[1,128,2240]{1,2,0:T(8,128)(2,1)} %collective-permute-done.8), channel_id=1, source_target_pairs={{0,1},{1,2},{2,3},{3,4},{4,5},{5,6},{6,7},{7,8},{8,9},{9,10},{10,1... | collective-permute-start | bytes 1720328 | tf_op jit(solution)/shard_map/ppermute | solution.py:207
  112.8 1.9 constant_dynamic-update-slice_fusion.1
  114.7 1.9 constant_dynamic-update-slice_fusion.7
  116.7 2.1 %copy.79 = bf16[1,128,2240]{2,1,0:T(8,128)(2,1)} copy(bf16[1,128,2240]{1,2,0:T(8,128)(2,1)} %collective-permute-done.4) | data formatting | bytes 1146880 | tf_op jit(solution)/shard_map/ppermute | solution.py:207
  118.8 3.2 %collective-permute-done.9 = bf16[1,128,2240]{1,2,0:T(8,128)(2,1)} collective-permute-done((bf16[1,128,2240]{1,2,0:T(8,128)(2,1)}, bf16[1,128,2240]{1,2,0:T(8,128)(2,1)}, u32[]{:S(2)}, u32[]{:S(2)}) %collective-permute-start.9) | collective-permute-done | bytes 573472 | tf_op jit(solution)/shard_map/ppermute | solution.py:207
  122.0 2.1 %copy.85 = bf16[1,128,2240]{2,1,0:T(8,128)(2,1)} copy(bf16[1,128,2240]{1,2,0:T(8,128)(2,1)} %collective-permute-done.9) | data formatting | bytes 1146880 | tf_op jit(solution)/shard_map/ppermute | solution.py:207
  124.2 1.9 constant_dynamic-update-slice_fusion.pk_ref
  126.1 1.9 constant_dynamic-update-slice_fusion.6.pv_ref
  132.1 57.0 %shard_map.142 = bf16[384,2240]{1,0:T(8,128)(2,1)S(1)} custom-call(s32[3]{0:T(128)S(1)} %copy-done.7, s32[18]{0:T(128)S(1)} %copy-done.5, s32[7]{0:T(128)S(1)} %copy-done.6, bf16[384,2240]{1,0:T(8,128)(2,1)S(1)} %copy.86.q_ref, bf16[128,2240]{1,0:T(8,128)(2,1)S(1)} %copy-done.3, bf16[128,2240]{1,0:T(8,128)(2,1)S(1)} %copy-done.4, ...), custom_call_target="tpu_custom_call" | custom-call | tf_op jit(solution)/shard_map/pallas_call | solution.py:159
  189.2 1.2 copy-done.1
  190.4 3.8 %copy.90 = bf16[384,2240]{0,1:T(8,128)(2,1)} copy(bf16[384,2240]{1,0:T(8,128)(2,1)} %copy-done.1) | data formatting | bytes 3440640
  194.2 2.2 %fusion.prior_ref = f32[32,2240]{1,0:T(8,128)S(1)} fusion(bf16[16,32,2240]{2,1,0:T(8,128)(2,1)} %bitcast.8, pred[16]{0:T(512)(128)(4,1)} %iota_compare_fusion.1), kind=kLoop, calls=%fused_computation.5 | loop fusion | flops 3368960 | bytes 2580496 | tf_op jit(solution)/shard_map/reduce_sum | solution.py:199
  198.5 2.2 %copy.89 = bf16[384,2240]{0,1:T(8,128)(2,1)} copy(bf16[384,2240]{1,0:T(8,128)(2,1)S(1)} %shard_map.141) | data formatting | bytes 3440640
  (67 shorter events, 15.4 us)
Async XLA Ops:
  7.2 25.8 %copy-start = (s32[16]{0:T(128)S(1)}, s32[16]{0:T(128)}, u32[]{:S(2)}) copy-start(s32[16]{0:T(128)} %param.21) | copy-start | bytes 196
  7.2 9.5 %copy-start.10 = (bf16[384,2240]{0,1:T(8,128)(2,1)S(1)}, bf16[384,2240]{0,1:T(8,128)(2,1)}, u32[]{:S(2)}) copy-start(bf16[384,2240]{0,1:T(8,128)(2,1)} %param.15) | copy-start | bytes 5160964
  7.2 187.0 %all-gather.3.cloned.1.call-start = ((), (), s32[]{:S(2)}) async-start(), calls=%async_computation | async-start | bytes 2506752 | tf_op jit(solution)/shard_map/all_gather | solution.py:197
  7.2 45.5 %collective-permute-start = (bf16[1,128,2240]{1,2,0:T(8,128)(2,1)}, bf16[1,128,2240]{1,2,0:T(8,128)(2,1)}, u32[]{:S(2)}, u32[]{:S(2)}) collective-permute-start(bf16[1,128,2240]{1,2,0:T(8,128)(2,1)} %param.17), channel_id=1, source_target_pairs={{0,1},{1,2},{2,3},{3,4},{4,5},{5,6},{6,7},{7,8},{8,9},{9,10},{10,1... | collective-permute-start | bytes 1720328 | tf_op jit(solution)/shard_map/ppermute | solution.py:207
  9.3 47.5 %collective-permute-start.5 = (bf16[1,128,2240]{1,2,0:T(8,128)(2,1)}, bf16[1,128,2240]{1,2,0:T(8,128)(2,1)}, u32[]{:S(2)}, u32[]{:S(2)}) collective-permute-start(bf16[1,128,2240]{1,2,0:T(8,128)(2,1)} %param.18), channel_id=1, source_target_pairs={{0,1},{1,2},{2,3},{3,4},{4,5},{5,6},{6,7},{7,8},{8,9},{9,10},{10,1... | collective-permute-start | bytes 1720328 | tf_op jit(solution)/shard_map/ppermute | solution.py:207
  16.7 16.0 %copy-start.13 = (bf16[1,128,2240]{1,2,0:T(8,128)(2,1)S(1)}, bf16[1,128,2240]{1,2,0:T(8,128)(2,1)}, u32[]{:S(2)}) copy-start(bf16[1,128,2240]{1,2,0:T(8,128)(2,1)} %param.17) | copy-start | bytes 1720324
  19.0 14.6 %copy-start.8 = (s32[16]{0:T(128)S(1)}, s32[16]{0:T(128)}, u32[]{:S(2)}) copy-start(s32[16]{0:T(128)} %param.22) | copy-start | bytes 196
  19.0 15.2 %copy-start.16 = (s32[16,3]{0,1:T(4,128)S(1)}, s32[16,3]{0,1:T(4,128)}, u32[]{:S(2)}) copy-start(s32[16,3]{0,1:T(4,128)} %param.24) | copy-start | bytes 580
  19.0 17.7 %copy-start.14 = (bf16[1,128,2240]{1,2,0:T(8,128)(2,1)S(1)}, bf16[1,128,2240]{1,2,0:T(8,128)(2,1)}, u32[]{:S(2)}) copy-start(bf16[1,128,2240]{1,2,0:T(8,128)(2,1)} %param.18) | copy-start | bytes 1720324
  31.0 7.5 %copy-start.9 = (s32[16]{0:T(128)S(1)}, s32[16]{0:T(128)}, u32[]{:S(2)}) copy-start(s32[16]{0:T(128)} %param.23) | copy-start | bytes 196
  33.6 8.7 %copy-start.11 = (bf16[128,2240]{0,1:T(8,128)(2,1)S(1)}, bf16[128,2240]{0,1:T(8,128)(2,1)}, u32[]{:S(2)}) copy-start(bf16[128,2240]{0,1:T(8,128)(2,1)} %param.19) | copy-start | bytes 1720324
  35.0 0.6 copy-start.15
  35.8 7.6 %copy-start.12 = (bf16[128,2240]{0,1:T(8,128)(2,1)S(1)}, bf16[128,2240]{0,1:T(8,128)(2,1)}, u32[]{:S(2)}) copy-start(bf16[128,2240]{0,1:T(8,128)(2,1)} %param.20) | copy-start | bytes 1720324
  52.7 17.7 %collective-permute-start.1 = (bf16[1,128,2240]{1,2,0:T(8,128)(2,1)}, bf16[1,128,2240]{1,2,0:T(8,128)(2,1)}, u32[]{:S(2)}, u32[]{:S(2)}) collective-permute-start(bf16[1,128,2240]{1,2,0:T(8,128)(2,1)} %collective-permute-done), channel_id=1, source_target_pairs={{0,1},{1,2},{2,3},{3,4},{4,5},{5,6},{6,7},{7,8},{8,9},{9,10},{10,1... | collective-permute-start | bytes 1720328 | tf_op jit(solution)/shard_map/ppermute | solution.py:207
  56.8 19.7 %collective-permute-start.6 = (bf16[1,128,2240]{1,2,0:T(8,128)(2,1)}, bf16[1,128,2240]{1,2,0:T(8,128)(2,1)}, u32[]{:S(2)}, u32[]{:S(2)}) collective-permute-start(bf16[1,128,2240]{1,2,0:T(8,128)(2,1)} %collective-permute-done.5), channel_id=1, source_target_pairs={{0,1},{1,2},{2,3},{3,4},{4,5},{5,6},{6,7},{7,8},{8,9},{9,10},{10,1... | collective-permute-start | bytes 1720328 | tf_op jit(solution)/shard_map/ppermute | solution.py:207
  72.5 14.3 %collective-permute-start.2 = (bf16[1,128,2240]{1,2,0:T(8,128)(2,1)}, bf16[1,128,2240]{1,2,0:T(8,128)(2,1)}, u32[]{:S(2)}, u32[]{:S(2)}) collective-permute-start(bf16[1,128,2240]{1,2,0:T(8,128)(2,1)} %collective-permute-done.1), channel_id=1, source_target_pairs={{0,1},{1,2},{2,3},{3,4},{4,5},{5,6},{6,7},{7,8},{8,9},{9,10},{10,1... | collective-permute-start | bytes 1720328 | tf_op jit(solution)/shard_map/ppermute | solution.py:207
  78.7 15.5 %collective-permute-start.7 = (bf16[1,128,2240]{1,2,0:T(8,128)(2,1)}, bf16[1,128,2240]{1,2,0:T(8,128)(2,1)}, u32[]{:S(2)}, u32[]{:S(2)}) collective-permute-start(bf16[1,128,2240]{1,2,0:T(8,128)(2,1)} %collective-permute-done.6), channel_id=1, source_target_pairs={{0,1},{1,2},{2,3},{3,4},{4,5},{5,6},{6,7},{7,8},{8,9},{9,10},{10,1... | collective-permute-start | bytes 1720328 | tf_op jit(solution)/shard_map/ppermute | solution.py:207
  88.9 13.2 %collective-permute-start.3 = (bf16[1,128,2240]{1,2,0:T(8,128)(2,1)}, bf16[1,128,2240]{1,2,0:T(8,128)(2,1)}, u32[]{:S(2)}, u32[]{:S(2)}) collective-permute-start(bf16[1,128,2240]{1,2,0:T(8,128)(2,1)} %collective-permute-done.2), channel_id=1, source_target_pairs={{0,1},{1,2},{2,3},{3,4},{4,5},{5,6},{6,7},{7,8},{8,9},{9,10},{10,1... | collective-permute-start | bytes 1720328 | tf_op jit(solution)/shard_map/ppermute | solution.py:207
  96.3 12.2 %collective-permute-start.8 = (bf16[1,128,2240]{1,2,0:T(8,128)(2,1)}, bf16[1,128,2240]{1,2,0:T(8,128)(2,1)}, u32[]{:S(2)}, u32[]{:S(2)}) collective-permute-start(bf16[1,128,2240]{1,2,0:T(8,128)(2,1)} %collective-permute-done.7), channel_id=1, source_target_pairs={{0,1},{1,2},{2,3},{3,4},{4,5},{5,6},{6,7},{7,8},{8,9},{9,10},{10,1... | collective-permute-start | bytes 1720328 | tf_op jit(solution)/shard_map/ppermute | solution.py:207
  104.2 12.4 %collective-permute-start.4 = (bf16[1,128,2240]{1,2,0:T(8,128)(2,1)}, bf16[1,128,2240]{1,2,0:T(8,128)(2,1)}, u32[]{:S(2)}, u32[]{:S(2)}) collective-permute-start(bf16[1,128,2240]{1,2,0:T(8,128)(2,1)} %collective-permute-done.3), channel_id=1, source_target_pairs={{0,1},{1,2},{2,3},{3,4},{4,5},{5,6},{6,7},{7,8},{8,9},{9,10},{10,1... | collective-permute-start | bytes 1720328 | tf_op jit(solution)/shard_map/ppermute | solution.py:207
  110.7 11.3 %collective-permute-start.9 = (bf16[1,128,2240]{1,2,0:T(8,128)(2,1)}, bf16[1,128,2240]{1,2,0:T(8,128)(2,1)}, u32[]{:S(2)}, u32[]{:S(2)}) collective-permute-start(bf16[1,128,2240]{1,2,0:T(8,128)(2,1)} %collective-permute-done.8), channel_id=1, source_target_pairs={{0,1},{1,2},{2,3},{3,4},{4,5},{5,6},{6,7},{7,8},{8,9},{9,10},{10,1... | collective-permute-start | bytes 1720328 | tf_op jit(solution)/shard_map/ppermute | solution.py:207
  128.0 1.1 copy-start.3
  129.1 1.1 copy-start.4
  130.2 0.7 copy-start.5
  130.8 0.6 copy-start.6
  131.5 0.7 copy-start.7
  189.2 1.3 copy-start.1
  196.5 1.0 copy-start.2
Sparse Core Ops, SparseCore 0:
  32.8 43.8 all-gather.2

commit v2 on v1

v2 whole, which is shorter than its diff:
```python
import functools
import math

import jax
import jax.numpy as jnp
from jax import lax
from jax.experimental import pallas as pl
from jax.experimental.pallas import tpu as pltpu
from jax.sharding import PartitionSpec as P

HD = 32
SPAN = 6
PAIR = 2 * HD
NEG = -1e30
VMEM_BYTES = 56 * 1024 * 1024


def head_groups(width):
    heads = width // HD
    return next(heads // n for n in (10, 14, 8, 6, 4, 2) if heads % n == 0)


def state_kernel(k_ref, v_ref, s_ref):
    size = k_ref.shape[0]
    full = lax.dot_general(
        v_ref[...], jnp.maximum(k_ref[...], 0), (((1,), (1,)), ((), ())),
        preferred_element_type=jnp.float32,
    )
    lane_head = lax.broadcasted_iota(jnp.int32, (HD, size), 1) // HD
    total = full[:HD, :]
    for h in range(1, size // HD):
        total = jnp.where(lane_head == h, full[h * HD : (h + 1) * HD, :], total)
    s_ref[0] = total


def stretch_states(keys, values):
    width, rows = keys.shape
    steps = head_groups(width)
    size = width // steps
    spec = pl.BlockSpec((size, rows), lambda g: (g, 0))
    return pl.pallas_call(
        state_kernel,
        grid=(steps,),
        in_specs=[spec, spec],
        out_specs=pl.BlockSpec((1, HD, size), lambda g: (g, 0, 0)),
        out_shape=jax.ShapeDtypeStruct((steps, HD, size), jnp.float32),
    )(keys, values)


def mix_kernel(q_ref, own_ref, prior_ref, gain_ref, o_ref, raw_ref):
    steps, _, size = own_ref.shape
    rows = q_ref.shape[1]
    width = steps * size
    row_head = lax.broadcasted_iota(jnp.int32, (size, size), 0) // HD
    lane_head = lax.broadcasted_iota(jnp.int32, (size, size), 1) // HD
    square = jnp.zeros((8, rows), jnp.float32)
    for g in range(steps):
        part = pl.ds(g * size, size)
        small = (own_ref[g] + prior_ref[g]).astype(jnp.bfloat16)
        tall = jnp.concatenate([small] * (size // HD), axis=0)
        weights = jnp.where(row_head == lane_head, tall, jnp.zeros_like(tall))
        raw = jnp.dot(
            weights, jnp.maximum(q_ref[part, :], 0), preferred_element_type=jnp.float32
        )
        raw_ref[part, :] = raw
        square = square + jnp.sum((raw * raw).reshape(size // 8, 8, rows), axis=0)
    total = jnp.sum(square, axis=0, keepdims=True)
    scale = lax.rsqrt(total * (1.0 / width) + 1e-05)
    for g in range(steps):
        part = pl.ds(g * size, size)
        o_ref[part, :] = (raw_ref[part, :] * scale * gain_ref[part, :]).astype(o_ref.dtype)


def self_mix(queries, own, prior, gain):
    width, rows = queries.shape
    return pl.pallas_call(
        mix_kernel,
        out_shape=jax.ShapeDtypeStruct((width, rows), jnp.bfloat16),
        scratch_shapes=[pltpu.VMEM((width, rows), jnp.float32)],
        compiler_params=pltpu.CompilerParams(vmem_limit_bytes=VMEM_BYTES),
    )(queries, own, prior, gain[:, None])


def attend_kernel(
    slots, tile_rows, tiles, least,
    seen_ref, list_ref, count_ref,
    q_ref, ck_ref, cv_ref, pk_ref, pv_ref, nk_ref, nv_ref, o_ref, k_buf, v_buf,
):
    size = q_ref.shape[0]
    pairs = size // PAIR
    sources = [(ck_ref, cv_ref), (pk_ref, pv_ref)]
    sources += [(nk_ref.at[r], nv_ref.at[r]) for r in range(SPAN - 1)]
    for b, (keys, values) in enumerate(sources):
        for p in range(pairs):
            k_buf[b, p] = keys[pl.ds(p * PAIR, PAIR), :].T
        v_buf[b] = values[...]
    factor = HD ** (-0.5) * math.log2(math.e)
    row = lax.broadcasted_iota(jnp.int32, (slots - least, 2 * tile_rows), 0) + least
    empty = jnp.zeros((HD, tile_rows), jnp.bfloat16)

    def tile(t, blocks):
        columns = pl.ds(pl.multiple_of(t * tile_rows, tile_rows), tile_rows)
        ids = [0] + [list_ref[t * SPAN + i] for i in range(blocks - 1)]
        counts = [None] + [count_ref[ids[i]] for i in range(1, blocks)]
        for p in range(pairs):
            q = q_ref[pl.ds(p * PAIR, PAIR), columns]
            both = jnp.concatenate(
                [
                    jnp.concatenate([q[:HD], empty], axis=1),
                    jnp.concatenate([empty, q[HD:]], axis=1),
                ],
                axis=0,
            )
            scores = []
            peak = None
            for i in range(blocks):
                s = jnp.dot(k_buf[ids[i], p], both, preferred_element_type=jnp.float32)
                if i:
                    s = jnp.concatenate(
                        [s[:least], jnp.where(row < counts[i], s[least:], NEG)], axis=0
                    )
                top = jnp.max(s.reshape(slots // 8, 8, 2 * tile_rows), axis=0)
                peak = top if peak is None else jnp.maximum(peak, top)
                scores.append(s)
            peak = jnp.max(peak, axis=0, keepdims=True)
            denom = None
            acc = None
            for i in range(blocks):
                e = jnp.exp2((scores[i] - peak) * factor)
                part = jnp.sum(e.reshape(slots // 8, 8, 2 * tile_rows), axis=0)
                denom = part if denom is None else denom + part
                added = jnp.dot(
                    v_buf[ids[i], pl.ds(p * PAIR, PAIR), :], e.astype(jnp.bfloat16),
                    preferred_element_type=jnp.float32,
                )
                acc = added if acc is None else acc + added
            inverse = 1.0 / jnp.sum(denom, axis=0, keepdims=True)
            mixed = jnp.concatenate(
                [
                    acc[:HD, :tile_rows] * inverse[:, :tile_rows],
                    acc[HD:, tile_rows:] * inverse[:, tile_rows:],
                ],
                axis=0,
            )
            o_ref[pl.ds(p * PAIR, PAIR), columns] = mixed.astype(o_ref.dtype)

    @pl.loop(0, tiles)
    def _(t):
        for blocks in range(1, SPAN + 2):
            @pl.when(seen_ref[t] == blocks - 1)
            def _():
                tile(t, blocks)


def cross_mix(queries, caption, prompt, near, seen, order, counts):
    width, rows = queries.shape
    slots = caption[0].shape[1]
    tiles = seen.shape[0]
    steps = head_groups(width)
    size = width // steps
    token = pl.BlockSpec((size, rows), lambda g, *_: (g, 0))
    block = pl.BlockSpec((size, slots), lambda g, *_: (g, 0))
    stack = pl.BlockSpec((SPAN - 1, size, slots), lambda g, *_: (0, g, 0))
    return pl.pallas_call(
        functools.partial(attend_kernel, slots, rows // tiles, tiles, slots * 5 // 8),
        grid_spec=pltpu.PrefetchScalarGridSpec(
            num_scalar_prefetch=3,
            grid=(steps,),
            in_specs=[token, block, block, block, block, stack, stack],
            out_specs=token,
            scratch_shapes=[
                pltpu.VMEM((SPAN + 1, size // PAIR, slots, PAIR), jnp.bfloat16),
                pltpu.VMEM((SPAN + 1, size, slots), jnp.bfloat16),
            ],
        ),
        out_shape=jax.ShapeDtypeStruct((width, rows), jnp.bfloat16),
        compiler_params=pltpu.CompilerParams(vmem_limit_bytes=VMEM_BYTES),
    )(seen, order, counts, queries, *caption, *prompt, *near)


def tables(stretch, span_start, span_end, prompt_tokens, region_mask):
    reach = jnp.arange(SPAN, dtype=jnp.int32)
    owner = stretch - reach
    row = jnp.maximum(owner, 0)
    covers = (owner >= 0) & (span_start[row] <= stretch) & (stretch < span_end[row])
    flags = (covers[:, None] & (region_mask[row] == 1)).T.astype(jnp.int32)
    seen = jnp.sum(flags, axis=1)
    place = jnp.cumsum(flags, axis=1) - 1
    hit = (place[:, :, None] == reach[None, None, :]) & (flags[:, :, None] == 1)
    order = jnp.sum(jnp.where(hit, reach[None, :, None] + 1, 0), axis=1)
    counts = jnp.concatenate([jnp.zeros((1,), jnp.int32), prompt_tokens[row]])
    return seen, order.reshape(-1), counts


def local(
    queries, keys, values, cross_queries, prompt_keys, prompt_values, caption_keys,
    caption_values, span_start, span_end, prompt_tokens, region_mask, out_gain,
):
    stretch = lax.axis_index("tm")
    devices = lax.axis_size("tm")
    own = stretch_states(keys.T, values.T)
    gathered = lax.all_gather(own.astype(jnp.bfloat16), "tm")
    earlier = jnp.arange(devices) < stretch
    prior = jnp.sum(
        jnp.where(earlier[:, None, None, None], gathered.astype(jnp.float32), 0.0), axis=0
    )
    self_mixed = self_mix(queries.T, own, prior, out_gain)
    prompt = (prompt_keys[0].T, prompt_values[0].T)
    route = [(i - 1, i) for i in range(1, devices)]
    moving = prompt
    blocks = []
    for _ in range(1, SPAN):
        moving = lax.ppermute(moving, "tm", route)
        blocks.append(moving)
    near = tuple(jnp.stack([b[i] for b in blocks], axis=0) for i in range(2))
    seen, order, counts = tables(stretch, span_start, span_end, prompt_tokens, region_mask)
    cross_mixed = cross_mix(
        cross_queries.T, (caption_keys.T, caption_values.T), prompt, near, seen, order, counts
    )
    return (self_mixed.T, cross_mixed.T)


def solution(mesh):
    rows = P(("groups", "tm"), None)
    blocks = P(("groups", "tm"), None, None)
    in_specs = (
        rows, rows, rows, rows, blocks, blocks, P("groups", None), P("groups", None),
        P("groups"), P("groups"), P("groups"), P("groups", None), P(),
    )
    return jax.shard_map(
        local, mesh=mesh, in_specs=in_specs, out_specs=(rows, rows), check_vma=False
    )
```

time: 211 us -> 160 us (0.76)
  the two profiles are of different devices: /device:TPU:20 before, /device:TPU:24 now
where the time goes in v2:
time: 160 us; the launch traced here: 161 us
  Pallas kernels  58.6 us (37%)
  waiting for transfers between devices  54.2 us (34%)
  starting transfers between devices  20.8 us (13%)
  between operations  14.3 us (9%)
  local copies, waits for them, and re-layouts  7.14 us (4%)
  other arithmetic  6.32 us (4%)
    ppermute x10, waiting for transfers between devices, local(): moving = lax.ppermute(moving, 'tm', route)  54.2 us
    pallas_call x1, Pallas kernels, cross_mix(): pl.pallas_call(functools.partial(attend_kernel, slots, rows // tiles, til...  47.1 us
    ppermute x10, starting transfers between devices, local(): moving = lax.ppermute(moving, 'tm', route)  20.7 us
    pallas_call x1, Pallas kernels, stretch_states(): pl.pallas_call(state_kernel, grid=(steps,), in_specs=[spec, spec], out_sp...  6.34 us
    pallas_call x1, Pallas kernels, self_mix(): pl.pallas_call(mix_kernel, out_shape=jax.ShapeDtypeStruct((width, rows),...  5.11 us
    reduce_sum x1, other arithmetic, local(): jnp.sum(jnp.where(earlier[:, None, None, None], gathered.astype(jnp.float...  3.22 us
  transfers between devices with their start and end apart: 11, of which 8 were waited for; matrix products, arithmetic and copies ran while one was open for 5% of the time, Pallas kernels for 33%

profile of v2, /device:TPU:24, one launch (start us, length us, event | category | flops | bytes accessed | tf_op | source)
XLA Modules:
  0.0 161.3 jit_solution(13942155595299295889)
XLA Ops:
  7.2 0.0 copy-start
  7.2 0.0 all-gather.3.cloned.1.call-start
  7.3 1.9 %collective-permute-start.5 = (bf16[2240,128]{1,0:T(8,128)(2,1)}, bf16[2240,128]{1,0:T(8,128)(2,1)S(1)}, u32[]{:S(2)}, u32[]{:S(2)}) collective-permute-start(bf16[2240,128]{1,0:T(8,128)(2,1)} %bitcast.53), channel_id=1, source_target_pairs={{0,1},{1,2},{2,3},{3,4},{4,5},{5,6},{6,7},{7,8},{8,9},{9,10},{10,1... | collective-permute-start | bytes 1720328 | tf_op jit(solution)/shard_map/ppermute | solution.py:213
  9.2 3.5 %collective-permute-start = (bf16[2240,128]{1,0:T(8,128)(2,1)}, bf16[2240,128]{1,0:T(8,128)(2,1)S(1)}, u32[]{:S(2)}, u32[]{:S(2)}) collective-permute-start(bf16[2240,128]{1,0:T(8,128)(2,1)} %bitcast.51), channel_id=1, source_target_pairs={{0,1},{1,2},{2,3},{3,4},{4,5},{5,6},{6,7},{7,8},{8,9},{9,10},{10,1... | collective-permute-start | bytes 1720328 | tf_op jit(solution)/shard_map/ppermute | solution.py:213
  12.7 6.3 %shard_map.140.own_ref = f32[7,32,320]{2,1,0:T(8,128)} custom-call(bf16[2240,384]{1,0:T(8,128)(2,1)} %bitcast.45, bf16[2240,384]{1,0:T(8,128)(2,1)} %bitcast.46), custom_call_target="tpu_custom_call" | custom-call | tf_op jit(solution)/shard_map/pallas_call | solution.py:41
  19.1 1.7 %convert_element_type.12 = bf16[7,32,320]{2,1,0:T(8,128)(2,1)} convert(f32[7,32,320]{2,1,0:T(8,128)} %shard_map.140.own_ref) | non-fusion elementwise | flops 71680 | bytes 430080 | tf_op jit(solution)/shard_map/convert_element_type | solution.py:202
  20.7 0.0 all-gather.3.cloned.1.call-update
  20.8 0.6 gather_fusion
  21.5 0.6 gather_fusion.1
  22.1 0.1 copy.27
  22.2 0.6 gather_fusion.2
  22.8 0.1 broadcast_compare_fusion
  22.9 0.1 copy.28
  23.0 0.1 copy.29
  23.1 0.1 select_reduce_fusion
  23.2 0.6 reshape.46.list_ref
  23.8 0.6 gather_fusion.3
  24.5 1.5 broadcast_in_dim.42.gain_ref
  25.9 0.6 pad_add_fusion.count_ref
  26.6 0.6 convert_reduce_fusion.seen_ref
  27.1 1.9 %collective-permute-start.6 = (bf16[2240,128]{1,0:T(8,128)(2,1)S(1)}, bf16[2240,128]{1,0:T(8,128)(2,1)S(1)}, u32[]{:S(2)}, u32[]{:S(2)}) collective-permute-start(bf16[2240,128]{1,0:T(8,128)(2,1)S(1)} %collective-permute-done.5), channel_id=1, source_target_pairs={{0,1},{1,2},{2,3},{3,4},{4,5},{5,6},{6,7},{7,8},{8,9},{9,10},{10,1... | collective-permute-start | bytes 1720328 | tf_op jit(solution)/shard_map/ppermute | solution.py:213
  29.1 1.9 %collective-permute-start.1 = (bf16[2240,128]{1,0:T(8,128)(2,1)S(1)}, bf16[2240,128]{1,0:T(8,128)(2,1)S(1)}, u32[]{:S(2)}, u32[]{:S(2)}) collective-permute-start(bf16[2240,128]{1,0:T(8,128)(2,1)S(1)} %collective-permute-done), channel_id=1, source_target_pairs={{0,1},{1,2},{2,3},{3,4},{4,5},{5,6},{6,7},{7,8},{8,9},{9,10},{10,1... | collective-permute-start | bytes 1720328 | tf_op jit(solution)/shard_map/ppermute | solution.py:213
  31.1 12.2 %collective-permute-done.6 = bf16[2240,128]{1,0:T(8,128)(2,1)S(1)} collective-permute-done((bf16[2240,128]{1,0:T(8,128)(2,1)S(1)}, bf16[2240,128]{1,0:T(8,128)(2,1)S(1)}, u32[]{:S(2)}, u32[]{:S(2)}) %collective-permute-start.6) | collective-permute-done | bytes 573472 | tf_op jit(solution)/shard_map/ppermute | solution.py:213
  43.3 1.9 %collective-permute-start.7 = (bf16[2240,128]{1,0:T(8,128)(2,1)S(1)}, bf16[2240,128]{1,0:T(8,128)(2,1)S(1)}, u32[]{:S(2)}, u32[]{:S(2)}) collective-permute-start(bf16[2240,128]{1,0:T(8,128)(2,1)S(1)} %collective-permute-done.6), channel_id=1, source_target_pairs={{0,1},{1,2},{2,3},{3,4},{4,5},{5,6},{6,7},{7,8},{8,9},{9,10},{10,1... | collective-permute-start | bytes 1720328 | tf_op jit(solution)/shard_map/ppermute | solution.py:213
  45.2 0.1 bitcast_dynamic-update-slice_fusion.3
  45.3 4.3 %collective-permute-done.1 = bf16[2240,128]{1,0:T(8,128)(2,1)S(1)} collective-permute-done((bf16[2240,128]{1,0:T(8,128)(2,1)S(1)}, bf16[2240,128]{1,0:T(8,128)(2,1)S(1)}, u32[]{:S(2)}, u32[]{:S(2)}) %collective-permute-start.1) | collective-permute-done | bytes 573472 | tf_op jit(solution)/shard_map/ppermute | solution.py:213
  49.6 1.9 %collective-permute-start.2 = (bf16[2240,128]{1,0:T(8,128)(2,1)S(1)}, bf16[2240,128]{1,0:T(8,128)(2,1)S(1)}, u32[]{:S(2)}, u32[]{:S(2)}) collective-permute-start(bf16[2240,128]{1,0:T(8,128)(2,1)S(1)} %collective-permute-done.1), channel_id=1, source_target_pairs={{0,1},{1,2},{2,3},{3,4},{4,5},{5,6},{6,7},{7,8},{8,9},{9,10},{10,1... | collective-permute-start | bytes 1720328 | tf_op jit(solution)/shard_map/ppermute | solution.py:213
  51.5 0.1 bitcast_dynamic-update-slice_fusion.8
  51.6 14.3 %collective-permute-done.7 = bf16[2240,128]{1,0:T(8,128)(2,1)S(1)} collective-permute-done((bf16[2240,128]{1,0:T(8,128)(2,1)S(1)}, bf16[2240,128]{1,0:T(8,128)(2,1)S(1)}, u32[]{:S(2)}, u32[]{:S(2)}) %collective-permute-start.7) | collective-permute-done | bytes 573472 | tf_op jit(solution)/shard_map/ppermute | solution.py:213
  66.0 1.9 %collective-permute-start.8 = (bf16[2240,128]{1,0:T(8,128)(2,1)S(1)}, bf16[2240,128]{1,0:T(8,128)(2,1)S(1)}, u32[]{:S(2)}, u32[]{:S(2)}) collective-permute-start(bf16[2240,128]{1,0:T(8,128)(2,1)S(1)} %collective-permute-done.7), channel_id=1, source_target_pairs={{0,1},{1,2},{2,3},{3,4},{4,5},{5,6},{6,7},{7,8},{8,9},{9,10},{10,1... | collective-permute-start | bytes 1720328 | tf_op jit(solution)/shard_map/ppermute | solution.py:213
  67.9 4.9 %collective-permute-done.2 = bf16[2240,128]{1,0:T(8,128)(2,1)S(1)} collective-permute-done((bf16[2240,128]{1,0:T(8,128)(2,1)S(1)}, bf16[2240,128]{1,0:T(8,128)(2,1)S(1)}, u32[]{:S(2)}, u32[]{:S(2)}) %collective-permute-start.2) | collective-permute-done | bytes 573472 | tf_op jit(solution)/shard_map/ppermute | solution.py:213
  72.8 1.9 %collective-permute-start.3 = (bf16[2240,128]{1,0:T(8,128)(2,1)S(1)}, bf16[2240,128]{1,0:T(8,128)(2,1)S(1)}, u32[]{:S(2)}, u32[]{:S(2)}) collective-permute-start(bf16[2240,128]{1,0:T(8,128)(2,1)S(1)} %collective-permute-done.2), channel_id=1, source_target_pairs={{0,1},{1,2},{2,3},{3,4},{4,5},{5,6},{6,7},{7,8},{8,9},{9,10},{10,1... | collective-permute-start | bytes 1720328 | tf_op jit(solution)/shard_map/ppermute | solution.py:213
  74.7 0.1 bitcast_dynamic-update-slice_fusion.2
  74.8 0.1 bitcast_dynamic-update-slice_fusion.7
  74.9 4.1 %collective-permute-done.8 = bf16[2240,128]{1,0:T(8,128)(2,1)S(1)} collective-permute-done((bf16[2240,128]{1,0:T(8,128)(2,1)S(1)}, bf16[2240,128]{1,0:T(8,128)(2,1)S(1)}, u32[]{:S(2)}, u32[]{:S(2)}) %collective-permute-start.8) | collective-permute-done | bytes 573472 | tf_op jit(solution)/shard_map/ppermute | solution.py:213
  78.9 1.9 %collective-permute-start.9 = (bf16[2240,128]{1,0:T(8,128)(2,1)S(1)}, bf16[2240,128]{1,0:T(8,128)(2,1)S(1)}, u32[]{:S(2)}, u32[]{:S(2)}) collective-permute-start(bf16[2240,128]{1,0:T(8,128)(2,1)S(1)} %collective-permute-done.8), channel_id=1, source_target_pairs={{0,1},{1,2},{2,3},{3,4},{4,5},{5,6},{6,7},{7,8},{8,9},{9,10},{10,1... | collective-permute-start | bytes 1720328 | tf_op jit(solution)/shard_map/ppermute | solution.py:213
  80.8 4.2 %collective-permute-done.3 = bf16[2240,128]{1,0:T(8,128)(2,1)S(1)} collective-permute-done((bf16[2240,128]{1,0:T(8,128)(2,1)S(1)}, bf16[2240,128]{1,0:T(8,128)(2,1)S(1)}, u32[]{:S(2)}, u32[]{:S(2)}) %collective-permute-start.3) | collective-permute-done | bytes 573472 | tf_op jit(solution)/shard_map/ppermute | solution.py:213
  85.1 1.9 %collective-permute-start.4 = (bf16[2240,128]{1,0:T(8,128)(2,1)S(1)}, bf16[2240,128]{1,0:T(8,128)(2,1)S(1)}, u32[]{:S(2)}, u32[]{:S(2)}) collective-permute-start(bf16[2240,128]{1,0:T(8,128)(2,1)S(1)} %collective-permute-done.3), channel_id=1, source_target_pairs={{0,1},{1,2},{2,3},{3,4},{4,5},{5,6},{6,7},{7,8},{8,9},{9,10},{10,1... | collective-permute-start | bytes 1720328 | tf_op jit(solution)/shard_map/ppermute | solution.py:213
  87.0 0.1 bitcast_dynamic-update-slice_fusion.1
  87.1 0.1 bitcast_dynamic-update-slice_fusion.6
  87.1 4.1 %collective-permute-done.9 = bf16[2240,128]{1,0:T(8,128)(2,1)S(1)} collective-permute-done((bf16[2240,128]{1,0:T(8,128)(2,1)S(1)}, bf16[2240,128]{1,0:T(8,128)(2,1)S(1)}, u32[]{:S(2)}, u32[]{:S(2)}) %collective-permute-start.9) | collective-permute-done | bytes 573472 | tf_op jit(solution)/shard_map/ppermute | solution.py:213
  91.2 0.1 bitcast_dynamic-update-slice_fusion.nv_ref
  91.3 6.1 %collective-permute-done.4 = bf16[2240,128]{1,0:T(8,128)(2,1)S(1)} collective-permute-done((bf16[2240,128]{1,0:T(8,128)(2,1)S(1)}, bf16[2240,128]{1,0:T(8,128)(2,1)S(1)}, u32[]{:S(2)}, u32[]{:S(2)}) %collective-permute-start.4) | collective-permute-done | bytes 573472 | tf_op jit(solution)/shard_map/ppermute | solution.py:213
  97.4 0.1 bitcast_dynamic-update-slice_fusion.5.nk_ref
  97.4 1.6 copy-done.3
  99.0 47.1 %shard_map.142 = bf16[2240,384]{1,0:T(8,128)(2,1)} custom-call(s32[3]{0:T(128)} %convert_reduce_fusion.seen_ref, s32[18]{0:T(128)} %reshape.46.list_ref, s32[7]{0:T(128)} %pad_add_fusion.count_ref, bf16[2240,384]{1,0:T(8,128)(2,1)} %bitcast.43, bf16[2240,128]{1,0:T(8,128)(2,1)} %bitcast.49, bf16[2240,128]{1,0:T(8,128)(2,1)} %bitcast.50, ...), custom_call_target="tpu_custom_call" | custom-call | tf_op jit(solution)/shard_map/pallas_call | solution.py:164
  146.1 3.2 %fusion.prior_ref = f32[7,32,320]{2,1,0:T(8,128)} fusion(bf16[16,7,32,320]{3,2,1,0:T(8,128)(2,1)} %bitcast.42, pred[16]{0:T(512)(128)(4,1)S(1)} %iota_compare_fusion.1), kind=kLoop, calls=%fused_computation.5 | loop fusion | flops 3368960 | bytes 2580496 | tf_op jit(solution)/shard_map/reduce_sum | solution.py:204
  149.4 5.1 %shard_map.141 = bf16[2240,384]{1,0:T(8,128)(2,1)} custom-call(bf16[2240,384]{1,0:T(8,128)(2,1)} %bitcast.47, f32[7,32,320]{2,1,0:T(8,128)} %shard_map.140.own_ref, f32[7,32,320]{2,1,0:T(8,128)} %fusion.prior_ref, f32[2240,1]{1,0:T(8,128)} %broadcast_in_dim.42.gain_ref), custom_call_target="tpu_custom_call" | custom-call | tf_op jit(solution)/shard_map/pallas_call | solution.py:76
  (25 shorter events, 0.2 us)
Async XLA Ops:
  7.2 13.6 %copy-start = (s32[16]{0:T(128)S(1)}, s32[16]{0:T(128)}, u32[]{:S(2)}) copy-start(s32[16]{0:T(128)} %param.21) | copy-start | bytes 196
  7.2 14.3 %copy-start.1 = (s32[16]{0:T(128)S(1)}, s32[16]{0:T(128)}, u32[]{:S(2)}) copy-start(s32[16]{0:T(128)} %param.22) | copy-start | bytes 196
  7.2 14.9 %copy-start.6 = (s32[16,3]{0,1:T(4,128)S(1)}, s32[16,3]{0,1:T(4,128)}, u32[]{:S(2)}) copy-start(s32[16,3]{0,1:T(4,128)} %param.24) | copy-start | bytes 580
  7.2 16.6 %copy-start.2 = (s32[16]{0:T(128)S(1)}, s32[16]{0:T(128)}, u32[]{:S(2)}) copy-start(s32[16]{0:T(128)} %param.23) | copy-start | bytes 196
  7.2 138.9 %all-gather.3.cloned.1.call-start = ((), (), s32[]{:S(2)}) async-start(), calls=%async_computation | async-start | bytes 2924544 | tf_op jit(solution)/shard_map/all_gather | solution.py:202
  7.3 19.9 %collective-permute-start.5 = (bf16[2240,128]{1,0:T(8,128)(2,1)}, bf16[2240,128]{1,0:T(8,128)(2,1)S(1)}, u32[]{:S(2)}, u32[]{:S(2)}) collective-permute-start(bf16[2240,128]{1,0:T(8,128)(2,1)} %bitcast.53), channel_id=1, source_target_pairs={{0,1},{1,2},{2,3},{3,4},{4,5},{5,6},{6,7},{7,8},{8,9},{9,10},{10,1... | collective-permute-start | bytes 1720328 | tf_op jit(solution)/shard_map/ppermute | solution.py:213
  9.2 19.9 %collective-permute-start = (bf16[2240,128]{1,0:T(8,128)(2,1)}, bf16[2240,128]{1,0:T(8,128)(2,1)S(1)}, u32[]{:S(2)}, u32[]{:S(2)}) collective-permute-start(bf16[2240,128]{1,0:T(8,128)(2,1)} %bitcast.51), channel_id=1, source_target_pairs={{0,1},{1,2},{2,3},{3,4},{4,5},{5,6},{6,7},{7,8},{8,9},{9,10},{10,1... | collective-permute-start | bytes 1720328 | tf_op jit(solution)/shard_map/ppermute | solution.py:213
  12.7 11.7 %copy-start.5 = (f32[2240]{0:T(1024)S(1)}, f32[2240]{0:T(1024)}, u32[]{:S(2)}) copy-start(f32[2240]{0:T(1024)} %param.25) | copy-start | bytes 26884
  27.1 16.1 %collective-permute-start.6 = (bf16[2240,128]{1,0:T(8,128)(2,1)S(1)}, bf16[2240,128]{1,0:T(8,128)(2,1)S(1)}, u32[]{:S(2)}, u32[]{:S(2)}) collective-permute-start(bf16[2240,128]{1,0:T(8,128)(2,1)S(1)} %collective-permute-done.5), channel_id=1, source_target_pairs={{0,1},{1,2},{2,3},{3,4},{4,5},{5,6},{6,7},{7,8},{8,9},{9,10},{10,1... | collective-permute-start | bytes 1720328 | tf_op jit(solution)/shard_map/ppermute | solution.py:213
  29.1 20.5 %collective-permute-start.1 = (bf16[2240,128]{1,0:T(8,128)(2,1)S(1)}, bf16[2240,128]{1,0:T(8,128)(2,1)S(1)}, u32[]{:S(2)}, u32[]{:S(2)}) collective-permute-start(bf16[2240,128]{1,0:T(8,128)(2,1)S(1)} %collective-permute-done), channel_id=1, source_target_pairs={{0,1},{1,2},{2,3},{3,4},{4,5},{5,6},{6,7},{7,8},{8,9},{9,10},{10,1... | collective-permute-start | bytes 1720328 | tf_op jit(solution)/shard_map/ppermute | solution.py:213
  43.3 22.7 %collective-permute-start.7 = (bf16[2240,128]{1,0:T(8,128)(2,1)S(1)}, bf16[2240,128]{1,0:T(8,128)(2,1)S(1)}, u32[]{:S(2)}, u32[]{:S(2)}) collective-permute-start(bf16[2240,128]{1,0:T(8,128)(2,1)S(1)} %collective-permute-done.6), channel_id=1, source_target_pairs={{0,1},{1,2},{2,3},{3,4},{4,5},{5,6},{6,7},{7,8},{8,9},{9,10},{10,1... | collective-permute-start | bytes 1720328 | tf_op jit(solution)/shard_map/ppermute | solution.py:213
  49.6 23.1 %collective-permute-start.2 = (bf16[2240,128]{1,0:T(8,128)(2,1)S(1)}, bf16[2240,128]{1,0:T(8,128)(2,1)S(1)}, u32[]{:S(2)}, u32[]{:S(2)}) collective-permute-start(bf16[2240,128]{1,0:T(8,128)(2,1)S(1)} %collective-permute-done.1), channel_id=1, source_target_pairs={{0,1},{1,2},{2,3},{3,4},{4,5},{5,6},{6,7},{7,8},{8,9},{9,10},{10,1... | collective-permute-start | bytes 1720328 | tf_op jit(solution)/shard_map/ppermute | solution.py:213
  66.0 13.0 %collective-permute-start.8 = (bf16[2240,128]{1,0:T(8,128)(2,1)S(1)}, bf16[2240,128]{1,0:T(8,128)(2,1)S(1)}, u32[]{:S(2)}, u32[]{:S(2)}) collective-permute-start(bf16[2240,128]{1,0:T(8,128)(2,1)S(1)} %collective-permute-done.7), channel_id=1, source_target_pairs={{0,1},{1,2},{2,3},{3,4},{4,5},{5,6},{6,7},{7,8},{8,9},{9,10},{10,1... | collective-permute-start | bytes 1720328 | tf_op jit(solution)/shard_map/ppermute | solution.py:213
  72.8 12.3 %collective-permute-start.3 = (bf16[2240,128]{1,0:T(8,128)(2,1)S(1)}, bf16[2240,128]{1,0:T(8,128)(2,1)S(1)}, u32[]{:S(2)}, u32[]{:S(2)}) collective-permute-start(bf16[2240,128]{1,0:T(8,128)(2,1)S(1)} %collective-permute-done.2), channel_id=1, source_target_pairs={{0,1},{1,2},{2,3},{3,4},{4,5},{5,6},{6,7},{7,8},{8,9},{9,10},{10,1... | collective-permute-start | bytes 1720328 | tf_op jit(solution)/shard_map/ppermute | solution.py:213
  78.9 12.3 %collective-permute-start.9 = (bf16[2240,128]{1,0:T(8,128)(2,1)S(1)}, bf16[2240,128]{1,0:T(8,128)(2,1)S(1)}, u32[]{:S(2)}, u32[]{:S(2)}) collective-permute-start(bf16[2240,128]{1,0:T(8,128)(2,1)S(1)} %collective-permute-done.8), channel_id=1, source_target_pairs={{0,1},{1,2},{2,3},{3,4},{4,5},{5,6},{6,7},{7,8},{8,9},{9,10},{10,1... | collective-permute-start | bytes 1720328 | tf_op jit(solution)/shard_map/ppermute | solution.py:213
  85.1 12.3 %collective-permute-start.4 = (bf16[2240,128]{1,0:T(8,128)(2,1)S(1)}, bf16[2240,128]{1,0:T(8,128)(2,1)S(1)}, u32[]{:S(2)}, u32[]{:S(2)}) collective-permute-start(bf16[2240,128]{1,0:T(8,128)(2,1)S(1)} %collective-permute-done.3), channel_id=1, source_target_pairs={{0,1},{1,2},{2,3},{3,4},{4,5},{5,6},{6,7},{7,8},{8,9},{9,10},{10,1... | collective-permute-start | bytes 1720328 | tf_op jit(solution)/shard_map/ppermute | solution.py:213
  91.3 6.2 %copy-start.4 = (bf16[5,2240,128]{2,1,0:T(8,128)(2,1)}, bf16[5,2240,128]{2,1,0:T(8,128)(2,1)S(1)}, u32[]{:S(2)}) copy-start(bf16[5,2240,128]{2,1,0:T(8,128)(2,1)S(1)} %bitcast_dynamic-update-slice_fusion.nv_ref) | copy-start | bytes 8601604
  97.4 1.6 copy-start.3
Sparse Core Ops, SparseCore 0:
  20.9 47.0 all-gather.2

commit v3 on v2

--- a/solution.py
+++ b/solution.py
@@ -178,6 +178,116 @@
     )(seen, order, counts, queries, *caption, *prompt, *near)
 
 
+PLANE = 4
+PARTS = 2
+
+
+def spread_kernel(devices, pk_ref, pv_ref, nk_ref, nv_ref, send_sem, recv_sem):
+    me = lax.axis_index("tm")
+    spot = me % PLANE
+    odd = spot % 2 == 1
+    even = spot % 2 == 0
+    front = spot < 2
+    back = spot >= 2
+    rows = pk_ref.shape[0] // PARTS
+    items = 2 * PARTS
+
+    def piece(reach, k):
+        own, near = ((pk_ref, nk_ref), (pv_ref, nv_ref))[k % 2]
+        part = pl.ds((k // 2) * rows, rows)
+        return own.at[part, :] if reach == 0 else near.at[reach - 1, part, :]
+
+    def copy(source, target, reach, line, k):
+        return pltpu.make_async_remote_copy(
+            src_ref=piece(source, k),
+            dst_ref=piece(reach, k),
+            send_sem=send_sem.at[line, k],
+            recv_sem=recv_sem.at[reach - 1, k],
+            device_id={"tm": target},
+            device_id_type=pl.DeviceIdType.MESH,
+        )
+
+    partner = jnp.where(front, me + 2, me - 2)
+    greeted = (
+        (partner, None), (me + 1, me + 1 < devices), (me - 1, me >= 1),
+        (me + PLANE, me + PLANE < devices), (me - PLANE, me >= PLANE),
+    )
+    barrier = pltpu.get_barrier_semaphore()
+    for target, there in greeted:
+        def hello(target=target):
+            pl.semaphore_signal(
+                barrier, inc=1, device_id={"tm": target}, device_id_type=pl.DeviceIdType.MESH
+            )
+        hello() if there is None else pl.when(there)(hello)
+    peers = 1
+    for target, there in greeted[1:]:
+        peers = peers + jnp.where(there, 1, 0)
+    pl.semaphore_wait(barrier, peers)
+
+    own_lines = (
+        (0, me + PLANE, 4, 0, me + PLANE < devices),
+        (0, me + 2, 2, 1, front),
+        (0, me + 1, 1, 2, even),
+    )
+    far = me >= PLANE
+    far_lines = (
+        (4, me - 2, 2, 3, far & back),
+        (4, me + 1, 5, 4, far & (me + 1 < devices)),
+        (4, me - 1, 3, 5, far & odd),
+    )
+    mid = me >= 2
+    mid_lines = (
+        (2, me + 1, 3, 6, mid & even),
+        (2, me - 1, 1, 7, mid & odd),
+    )
+
+    def start(lines, k):
+        for source, target, reach, line, there in lines:
+            @pl.when(there)
+            def _():
+                copy(source, target, reach, line, k).start()
+
+    def arrived(reach, k):
+        @pl.when(me >= reach)
+        def _():
+            copy(reach, partner, reach, 0, k).wait_recv()
+
+    for k in range(items):
+        start(own_lines, k)
+    for k in range(items + 1):
+        if k < items:
+            arrived(4, k)
+            start(far_lines, k)
+        if k >= 1:
+            arrived(2, k - 1)
+            start(mid_lines, k - 1)
+    for k in range(items):
+        for reach in (1, 3, 5):
+            arrived(reach, k)
+    for k in range(items):
+        for source, target, reach, line, there in own_lines + far_lines + mid_lines:
+            @pl.when(there)
+            def _():
+                copy(source, target, reach, line, k).wait_send()
+
+
+def spread(prompt_keys, prompt_values, devices):
+    width, slots = prompt_keys.shape
+    stack = jax.ShapeDtypeStruct((SPAN - 1, width, slots), prompt_keys.dtype)
+    anywhere = pl.BlockSpec(memory_space=pl.ANY)
+    return pl.pallas_call(
+        functools.partial(spread_kernel, devices),
+        out_shape=(stack, stack),
+        in_specs=[anywhere, anywhere],
+        out_specs=(anywhere, anywhere),
+        scratch_shapes=[
+            pltpu.SemaphoreType.DMA((8, 2 * PARTS)),
+            pltpu.SemaphoreType.DMA((SPAN - 1, 2 * PARTS)),
+        ],
+        compiler_params=pltpu.CompilerParams(collective_id=0, has_side_effects=True),
+    )(prompt_keys, prompt_values)
+
+
 def tables(stretch, span_start, span_end, prompt_tokens, region_mask):
     reach = jnp.arange(SPAN, dtype=jnp.int32)
     owner = stretch - reach
@@ -206,13 +316,7 @@
     )
     self_mixed = self_mix(queries.T, own, prior, out_gain)
     prompt = (prompt_keys[0].T, prompt_values[0].T)
-    route = [(i - 1, i) for i in range(1, devices)]
-    moving = prompt
-    blocks = []
-    for _ in range(1, SPAN):
-        moving = lax.ppermute(moving, "tm", route)
-        blocks.append(moving)
-    near = tuple(jnp.stack([b[i] for b in blocks], axis=0) for i in range(2))
+    near = spread(*prompt, devices)
     seen, order, counts = tables(stretch, span_start, span_end, prompt_tokens, region_mask)
     cross_mixed = cross_mix(
         cross_queries.T, (caption_keys.T, caption_values.T), prompt, near, seen, order, counts

time: 160 us -> 145 us (0.906); the launches traced: 161 us -> 143 us
  Pallas kernels: 58.6 us -> 118 us
  waiting for transfers between devices: 54.2 us -> 0.04 us
  starting transfers between devices: 20.8 us -> 0.04 us
  local copies, waits for them, and re-layouts: 7.14 us -> 4.86 us
    pallas_call x0 -> x1, Pallas kernels: none -> 63.3 us  [spread(): pl.pallas_call(functools.partial(spread_kernel, devices), out_shape=(stac...]
    ppermute x10 -> x0, waiting for transfers between devices: 54.2 us -> none  [local(): moving = lax.ppermute(moving, 'tm', route)]
    ppermute x10 -> x0, starting transfers between devices: 20.7 us -> none  [local(): moving = lax.ppermute(moving, 'tm', route)]
    pallas_call x1, Pallas kernels: 47.1 us -> 42.9 us  [cross_mix(): pl.pallas_call(functools.partial(attend_kernel, slots, rows // tiles, til...]
    unnamed x23 -> x11, local copies, waits for them, and re-layouts: 2.21 us -> 0.11 us
  transfers between devices with their start and end apart: 11 -> 1, of which waited for: 8 -> 0; matrix products, arithmetic and copies ran while one was open for 5% -> 4% of each run, Pallas kernels for 33% -> 74%
where the time goes in v3:
time: 145 us; the launch traced here: 143 us
  Pallas kernels  118 us (81%)
  between operations  14.1 us (10%)
  other arithmetic  6.33 us (4%)
  local copies, waits for them, and re-layouts  4.86 us (3%)
    pallas_call x1, Pallas kernels, spread(): pl.pallas_call(functools.partial(spread_kernel, devices), out_shape=(stac...  63.3 us
    pallas_call x1, Pallas kernels, cross_mix(): pl.pallas_call(functools.partial(attend_kernel, slots, rows // tiles, til...  42.9 us
    pallas_call x1, Pallas kernels, stretch_states(): pl.pallas_call(state_kernel, grid=(steps,), in_specs=[spec, spec], out_sp...  6.34 us
    pallas_call x1, Pallas kernels, self_mix(): pl.pallas_call(mix_kernel, out_shape=jax.ShapeDtypeStruct((width, rows),...  5.11 us
    reduce_sum x1, other arithmetic, local(): jnp.sum(jnp.where(earlier[:, None, None, None], gathered.astype(jnp.float...  3.2 us
  transfers between devices with their start and end apart: 1, of which 0 were waited for; matrix products, arithmetic and copies ran while one was open for 4% of the time, Pallas kernels for 74%

profile of v3, /device:TPU:24, one launch (start us, length us, event | category | flops | bytes accessed | tf_op | source)
XLA Modules:
  0.0 143.1 jit_solution(14681250673743799325)
XLA Ops:
  7.2 0.0 copy-start
  7.2 0.0 all-gather.3.cloned.1.call-start
  7.2 0.0 copy-start.1
  7.2 6.3 %shard_map.140.own_ref = f32[7,32,320]{2,1,0:T(8,128)} custom-call(bf16[2240,384]{1,0:T(8,128)(2,1)} %bitcast.29, bf16[2240,384]{1,0:T(8,128)(2,1)} %bitcast.30), custom_call_target="tpu_custom_call" | custom-call | tf_op jit(solution)/shard_map/pallas_call | solution.py:41
  13.6 0.0 copy-start.4
  13.6 0.0 copy-start.2
  13.6 0.0 copy-start.3
  13.6 1.7 %convert_element_type.12 = bf16[7,32,320]{2,1,0:T(8,128)(2,1)} convert(f32[7,32,320]{2,1,0:T(8,128)} %shard_map.140.own_ref) | non-fusion elementwise | flops 71680 | bytes 430080 | tf_op jit(solution)/shard_map/convert_element_type | solution.py:312
  15.3 0.0 all-gather.3.cloned.1.call-update
  15.3 0.0 copy-done
  15.4 0.6 gather_fusion
  16.0 0.0 copy-done.1
  16.0 0.6 gather_fusion.1
  16.7 0.0 copy-done.4
  16.7 0.1 copy.27
  16.7 0.6 gather_fusion.2
  17.3 0.1 broadcast_compare_fusion
  17.4 0.1 copy.28
  17.5 0.1 copy.29
  17.6 0.1 select_reduce_fusion
  17.7 0.6 reshape.46.list_ref
  18.3 0.0 copy-done.2
  18.3 0.6 gather_fusion.3
  19.0 0.0 copy-done.3
  19.0 1.5 %broadcast_in_dim.42.gain_ref = f32[2240,1]{1,0:T(8,128)} reshape(f32[2240]{0:T(1024)S(1)} %copy-done.3) | data formatting | bytes 17920 | tf_op jit(solution)/shard_map/broadcast_in_dim | solution.py:81
  20.4 63.3 %shard_map.142 = (bf16[5,2240,128]{2,1,0:T(8,128)(2,1)}, bf16[5,2240,128]{2,1,0:T(8,128)(2,1)}) custom-call(bf16[2240,128]{1,0:T(8,128)(2,1)} %bitcast.23, bf16[2240,128]{1,0:T(8,128)(2,1)} %bitcast.25), custom_call_target="tpu_custom_call" | custom-call | tf_op jit(solution)/shard_map/pallas_call | solution.py:278
  83.8 0.6 pad_add_fusion.count_ref
  84.4 0.6 convert_reduce_fusion.seen_ref
  85.0 42.9 %shard_map.143 = bf16[2240,384]{1,0:T(8,128)(2,1)} custom-call(s32[3]{0:T(128)} %convert_reduce_fusion.seen_ref, s32[18]{0:T(128)} %reshape.46.list_ref, s32[7]{0:T(128)} %pad_add_fusion.count_ref, bf16[2240,384]{1,0:T(8,128)(2,1)} %bitcast.27, bf16[2240,128]{1,0:T(8,128)(2,1)} %bitcast.33, bf16[2240,128]{1,0:T(8,128)(2,1)} %bitcast.34, ...), custom_call_target="tpu_custom_call" | custom-call | tf_op jit(solution)/shard_map/pallas_call | solution.py:164
  127.9 0.0 all-gather.3.cloned.1.call-done
  127.9 3.2 %fusion.prior_ref = f32[7,32,320]{2,1,0:T(8,128)} fusion(bf16[16,7,32,320]{3,2,1,0:T(8,128)(2,1)} %bitcast.22, pred[16]{0:T(512)(128)(4,1)S(1)} %iota_compare_fusion.1), kind=kLoop, calls=%fused_computation.5 | loop fusion | flops 3368960 | bytes 2580496 | tf_op jit(solution)/shard_map/reduce_sum | solution.py:314
  131.1 5.1 %shard_map.141 = bf16[2240,384]{1,0:T(8,128)(2,1)} custom-call(bf16[2240,384]{1,0:T(8,128)(2,1)} %bitcast.31, f32[7,32,320]{2,1,0:T(8,128)} %shard_map.140.own_ref, f32[7,32,320]{2,1,0:T(8,128)} %fusion.prior_ref, f32[2240,1]{1,0:T(8,128)} %broadcast_in_dim.42.gain_ref), custom_call_target="tpu_custom_call" | custom-call | tf_op jit(solution)/shard_map/pallas_call | solution.py:76
  (8 shorter events, 0.1 us)
Async XLA Ops:
  7.2 8.2 %copy-start = (s32[16]{0:T(128)S(1)}, s32[16]{0:T(128)}, u32[]{:S(2)}) copy-start(s32[16]{0:T(128)} %param.21) | copy-start | bytes 196
  7.2 120.7 %all-gather.3.cloned.1.call-start = ((), (), s32[]{:S(2)}) async-start(), calls=%async_computation | async-start | bytes 2924544 | tf_op jit(solution)/shard_map/all_gather | solution.py:312
  7.2 8.8 %copy-start.1 = (s32[16]{0:T(128)S(1)}, s32[16]{0:T(128)}, u32[]{:S(2)}) copy-start(s32[16]{0:T(128)} %param.22) | copy-start | bytes 196
  13.6 3.1 %copy-start.4 = (s32[16,3]{0,1:T(4,128)S(1)}, s32[16,3]{0,1:T(4,128)}, u32[]{:S(2)}) copy-start(s32[16,3]{0,1:T(4,128)} %param.24) | copy-start | bytes 580
  13.6 4.8 %copy-start.2 = (s32[16]{0:T(128)S(1)}, s32[16]{0:T(128)}, u32[]{:S(2)}) copy-start(s32[16]{0:T(128)} %param.23) | copy-start | bytes 196
  13.6 5.4 %copy-start.3 = (f32[2240]{0:T(1024)S(1)}, f32[2240]{0:T(1024)}, u32[]{:S(2)}) copy-start(f32[2240]{0:T(1024)} %param.25) | copy-start | bytes 26884
Sparse Core Ops, SparseCore 0:
  15.4 50.9 all-gather.2

commit v4 on v3

--- a/solution.py
+++ b/solution.py
@@ -20,31 +20,17 @@
     return next(heads // n for n in (10, 14, 8, 6, 4, 2) if heads % n == 0)
 
 
-def state_kernel(k_ref, v_ref, s_ref):
-    size = k_ref.shape[0]
+def state_part(keys, values):
+    size = keys.shape[0]
     full = lax.dot_general(
-        v_ref[...], jnp.maximum(k_ref[...], 0), (((1,), (1,)), ((), ())),
+        values, jnp.maximum(keys, 0), (((1,), (1,)), ((), ())),
         preferred_element_type=jnp.float32,
     )
     lane_head = lax.broadcasted_iota(jnp.int32, (HD, size), 1) // HD
     total = full[:HD, :]
     for h in range(1, size // HD):
         total = jnp.where(lane_head == h, full[h * HD : (h + 1) * HD, :], total)
-    s_ref[0] = total
-
-
-def stretch_states(keys, values):
-    width, rows = keys.shape
-    steps = head_groups(width)
-    size = width // steps
-    spec = pl.BlockSpec((size, rows), lambda g: (g, 0))
-    return pl.pallas_call(
-        state_kernel,
-        grid=(steps,),
-        in_specs=[spec, spec],
-        out_specs=pl.BlockSpec((1, HD, size), lambda g: (g, 0, 0)),
-        out_shape=jax.ShapeDtypeStruct((steps, HD, size), jnp.float32),
-    )(keys, values)
+    return total
 
 
 def mix_kernel(q_ref, own_ref, prior_ref, gain_ref, o_ref, raw_ref):
@@ -182,7 +168,9 @@
 PARTS = 2
 
 
-def spread_kernel(devices, pk_ref, pv_ref, nk_ref, nv_ref, send_sem, recv_sem):
+def spread_kernel(
+    devices, pk_ref, pv_ref, k_ref, v_ref, nk_ref, nv_ref, own_ref, sent_ref, send_sem, recv_sem
+):
     me = lax.axis_index("tm")
     spot = me % PLANE
     odd = spot % 2 == 1
@@ -254,6 +242,12 @@
 
     for k in range(items):
         start(own_lines, k)
+    size = own_ref.shape[2]
+    for g in range(own_ref.shape[0]):
+        part = pl.ds(g * size, size)
+        state = state_part(k_ref[part, :], v_ref[part, :])
+        own_ref[g] = state
+        sent_ref[g] = state.astype(jnp.bfloat16)
     for k in range(items + 1):
         if k < items:
             arrived(4, k)
@@ -271,21 +265,29 @@
                 copy(source, target, reach, line, k).wait_send()
 
 
-def spread(prompt_keys, prompt_values, devices):
+def spread(prompt_keys, prompt_values, keys, values, devices):
     width, slots = prompt_keys.shape
     stack = jax.ShapeDtypeStruct((SPAN - 1, width, slots), prompt_keys.dtype)
+    steps = head_groups(width)
+    state = (steps, HD, width // steps)
     anywhere = pl.BlockSpec(memory_space=pl.ANY)
+    whole = pl.BlockSpec(memory_space=pltpu.VMEM)
     return pl.pallas_call(
         functools.partial(spread_kernel, devices),
-        out_shape=(stack, stack),
-        in_specs=[anywhere, anywhere],
-        out_specs=(anywhere, anywhere),
+        out_shape=(
+            stack, stack, jax.ShapeDtypeStruct(state, jnp.float32),
+            jax.ShapeDtypeStruct(state, jnp.bfloat16),
+        ),
+        in_specs=[anywhere, anywhere, whole, whole],
+        out_specs=(anywhere, anywhere, whole, whole),
         scratch_shapes=[
             pltpu.SemaphoreType.DMA((8, 2 * PARTS)),
             pltpu.SemaphoreType.DMA((SPAN - 1, 2 * PARTS)),
         ],
-        compiler_params=pltpu.CompilerParams(collective_id=0, has_side_effects=True),
-    )(prompt_keys, prompt_values)
+        compiler_params=pltpu.CompilerParams(
+            collective_id=0, has_side_effects=True, vmem_limit_bytes=VMEM_BYTES
+        ),
+    )(prompt_keys, prompt_values, keys, values)
 
 
 def tables(stretch, span_start, span_end, prompt_tokens, region_mask):
@@ -308,15 +310,14 @@
 ):
     stretch = lax.axis_index("tm")
     devices = lax.axis_size("tm")
-    own = stretch_states(keys.T, values.T)
-    gathered = lax.all_gather(own.astype(jnp.bfloat16), "tm")
+    prompt = (prompt_keys[0].T, prompt_values[0].T)
+    *near, own, sent = spread(*prompt, keys.T, values.T, devices)
+    gathered = lax.all_gather(sent, "tm")
     earlier = jnp.arange(devices) < stretch
     prior = jnp.sum(
         jnp.where(earlier[:, None, None, None], gathered.astype(jnp.float32), 0.0), axis=0
     )
     self_mixed = self_mix(queries.T, own, prior, out_gain)
-    prompt = (prompt_keys[0].T, prompt_values[0].T)
-    near = spread(*prompt, devices)
     seen, order, counts = tables(stretch, span_start, span_end, prompt_tokens, region_mask)
     cross_mixed = cross_mix(
         cross_queries.T, (caption_keys.T, caption_values.T), prompt, near, seen, order, counts

time: 145 us -> 127 us (0.88)
  the two profiles are of different devices: /device:TPU:24 before, /device:TPU:17 now
where the time goes in v4:
time: 127 us; the launch traced here: 125 us
  Pallas kernels  101 us (80%)
  between operations  14.1 us (11%)
  local copies, waits for them, and re-layouts  4.89 us (4%)
  other arithmetic  4.6 us (4%)
    pallas_call x1, Pallas kernels, spread(): pl.pallas_call(functools.partial(spread_kernel, devices), out_shape=(stac...  53.8 us
    pallas_call x1, Pallas kernels, cross_mix(): pl.pallas_call(functools.partial(attend_kernel, slots, rows // tiles, til...  42 us
    pallas_call x1, Pallas kernels, self_mix(): pl.pallas_call(mix_kernel, out_shape=jax.ShapeDtypeStruct((width, rows),...  5.11 us
    reduce_sum x1, other arithmetic, local(): jnp.sum(jnp.where(earlier[:, None, None, None], gathered.astype(jnp.float...  3.2 us
  transfers between devices with their start and end apart: 1, of which 0 were waited for; matrix products, arithmetic and copies ran while one was open for 5% of the time, Pallas kernels for 34%

profile of v4, /device:TPU:17, one launch (start us, length us, event | category | flops | bytes accessed | tf_op | source)
XLA Modules:
  0.0 124.6 jit_solution(8190469121684065463)
XLA Ops:
  7.2 0.0 copy-start
  7.2 0.0 all-gather.3.cloned.1.call-start
  7.2 0.0 copy-start.1
  7.2 0.0 copy-start.4
  7.2 0.0 copy-start.2
  7.3 53.8 %shard_map.140 = (bf16[5,2240,128]{2,1,0:T(8,128)(2,1)}, bf16[5,2240,128]{2,1,0:T(8,128)(2,1)}, f32[7,32,320]{2,1,0:T(8,128)}, bf16[7,32,320]{2,1,0:T(8,128)(2,1)}) custom-call(bf16[2240,128]{1,0:T(8,128)(2,1)} %bitcast.23, bf16[2240,128]{1,0:T(8,128)(2,1)} %bitcast.25, bf16[2240,384]{1,0:T(8,128)(2,1)} %bitcast.29, bf16[2240,384]{1,0:T(8,128)(2,1)} %bitcast.30), custom_call_target="tpu_custom_call" | custom-call | tf_op jit(solution)/shard_map/pallas_call | solution.py:275
  61.1 0.0 copy-start.3
  61.1 0.0 all-gather.3.cloned.1.call-update
  61.1 0.0 copy-done
  61.1 0.6 gather_fusion
  61.8 0.0 copy-done.1
  61.8 0.6 gather_fusion.1
  62.4 0.0 copy-done.4
  62.4 0.1 copy.27
  62.5 0.6 gather_fusion.2
  63.1 0.1 broadcast_compare_fusion
  63.2 0.1 copy.28
  63.3 0.1 copy.29
  63.4 0.1 select_reduce_fusion
  63.5 0.6 reshape.46.list_ref
  64.1 0.0 copy-done.2
  64.1 0.6 gather_fusion.3
  64.8 0.0 copy-done.3
  64.8 1.5 %broadcast_in_dim.42.gain_ref = f32[2240,1]{1,0:T(8,128)} reshape(f32[2240]{0:T(1024)S(1)} %copy-done.3) | data formatting | bytes 17920 | tf_op jit(solution)/shard_map/broadcast_in_dim | solution.py:67
  66.3 0.6 pad_add_fusion.count_ref
  66.9 0.5 convert_reduce_fusion.seen_ref
  67.4 42.0 %shard_map.142 = bf16[2240,384]{1,0:T(8,128)(2,1)} custom-call(s32[3]{0:T(128)} %convert_reduce_fusion.seen_ref, s32[18]{0:T(128)} %reshape.46.list_ref, s32[7]{0:T(128)} %pad_add_fusion.count_ref, bf16[2240,384]{1,0:T(8,128)(2,1)} %bitcast.27, bf16[2240,128]{1,0:T(8,128)(2,1)} %bitcast.33, bf16[2240,128]{1,0:T(8,128)(2,1)} %bitcast.34, ...), custom_call_target="tpu_custom_call" | custom-call | tf_op jit(solution)/shard_map/pallas_call | solution.py:150
  109.4 0.0 all-gather.3.cloned.1.call-done
  109.5 3.2 %fusion.prior_ref = f32[7,32,320]{2,1,0:T(8,128)} fusion(bf16[16,7,32,320]{3,2,1,0:T(8,128)(2,1)} %bitcast.22, pred[16]{0:T(512)(128)(4,1)S(1)} %iota_compare_fusion.1), kind=kLoop, calls=%fused_computation.5 | loop fusion | flops 3368960 | bytes 2580496 | tf_op jit(solution)/shard_map/reduce_sum | solution.py:317
  112.7 5.1 %shard_map.141 = bf16[2240,384]{1,0:T(8,128)(2,1)} custom-call(bf16[2240,384]{1,0:T(8,128)(2,1)} %bitcast.31, f32[7,32,320]{2,1,0:T(8,128)} %get-tuple-element.6.own_ref, f32[7,32,320]{2,1,0:T(8,128)} %fusion.prior_ref, f32[2240,1]{1,0:T(8,128)} %broadcast_in_dim.42.gain_ref), custom_call_target="tpu_custom_call" | custom-call | tf_op jit(solution)/shard_map/pallas_call | solution.py:62
  (8 shorter events, 0.1 us)
Async XLA Ops:
  7.2 54.0 %copy-start = (s32[16]{0:T(128)S(1)}, s32[16]{0:T(128)}, u32[]{:S(2)}) copy-start(s32[16]{0:T(128)} %param.21) | copy-start | bytes 196
  7.2 102.3 %all-gather.3.cloned.1.call-start = ((), (), s32[]{:S(2)}) async-start(), calls=%async_computation | async-start | bytes 2924544 | tf_op jit(solution)/shard_map/all_gather | solution.py:315
  7.2 54.6 %copy-start.1 = (s32[16]{0:T(128)S(1)}, s32[16]{0:T(128)}, u32[]{:S(2)}) copy-start(s32[16]{0:T(128)} %param.22) | copy-start | bytes 196
  7.2 55.2 %copy-start.4 = (s32[16,3]{0,1:T(4,128)S(1)}, s32[16,3]{0,1:T(4,128)}, u32[]{:S(2)}) copy-start(s32[16,3]{0,1:T(4,128)} %param.24) | copy-start | bytes 580
  7.2 56.9 %copy-start.2 = (s32[16]{0:T(128)S(1)}, s32[16]{0:T(128)}, u32[]{:S(2)}) copy-start(s32[16]{0:T(128)} %param.23) | copy-start | bytes 196
  61.1 3.7 %copy-start.3 = (f32[2240]{0:T(1024)S(1)}, f32[2240]{0:T(1024)}, u32[]{:S(2)}) copy-start(f32[2240]{0:T(1024)} %param.25) | copy-start | bytes 26884
Sparse Core Ops, SparseCore 0:
  61.2 42.7 all-gather.2

commit v5 on v4

--- a/solution.py
+++ b/solution.py
@@ -77,9 +77,11 @@
     sources = [(ck_ref, cv_ref), (pk_ref, pv_ref)]
     sources += [(nk_ref.at[r], nv_ref.at[r]) for r in range(SPAN - 1)]
     for b, (keys, values) in enumerate(sources):
-        for p in range(pairs):
-            k_buf[b, p] = keys[pl.ds(p * PAIR, PAIR), :].T
-        v_buf[b] = values[...]
+        def fill(b=b, keys=keys, values=values):
+            for p in range(pairs):
+                k_buf[b, p] = keys[pl.ds(p * PAIR, PAIR), :].T
+            v_buf[b] = values[...]
+        fill() if b == 0 else pl.when(count_ref[b] > 0)(fill)
     factor = HD ** (-0.5) * math.log2(math.e)
     row = lax.broadcasted_iota(jnp.int32, (slots - least, 2 * tile_rows), 0) + least
     empty = jnp.zeros((HD, tile_rows), jnp.bfloat16)
@@ -300,7 +302,9 @@
     place = jnp.cumsum(flags, axis=1) - 1
     hit = (place[:, :, None] == reach[None, None, :]) & (flags[:, :, None] == 1)
     order = jnp.sum(jnp.where(hit, reach[None, :, None] + 1, 0), axis=1)
-    counts = jnp.concatenate([jnp.zeros((1,), jnp.int32), prompt_tokens[row]])
+    counts = jnp.concatenate(
+        [jnp.zeros((1,), jnp.int32), jnp.where(flags.sum(axis=0) > 0, prompt_tokens[row], 0)]
+    )
     return seen, order.reshape(-1), counts
 
 

time: 127 us -> 129 us (1.016)
  the two profiles are of different devices: /device:TPU:17 before, /device:TPU:19 now
where the time goes in v5:
time: 129 us
  Pallas kernels  105 us (81%)
  between operations  14.1 us (11%)
  local copies, waits for them, and re-layouts  4.89 us (4%)
  other arithmetic  4.61 us (4%)
    pallas_call x1, Pallas kernels, spread(): pl.pallas_call(functools.partial(spread_kernel, devices), out_shape=(stac...  53.8 us
    pallas_call x1, Pallas kernels, cross_mix(): pl.pallas_call(functools.partial(attend_kernel, slots, rows // tiles, til...  45.9 us
    pallas_call x1, Pallas kernels, self_mix(): pl.pallas_call(mix_kernel, out_shape=jax.ShapeDtypeStruct((width, rows),...  5.11 us
    reduce_sum x1, other arithmetic, local(): jnp.sum(jnp.where(earlier[:, None, None, None], gathered.astype(jnp.float...  3.2 us
  transfers between devices with their start and end apart: 1, of which 0 were waited for; matrix products, arithmetic and copies ran while one was open for 5% of the time, Pallas kernels for 36%

profile of v5, /device:TPU:19, one launch (start us, length us, event | category | flops | bytes accessed | tf_op | source)
XLA Modules:
  0.0 128.5 jit_solution(4129453313115125605)
XLA Ops:
  7.2 0.0 copy-start
  7.2 0.0 all-gather.3.cloned.1.call-start
  7.2 0.0 copy-start.1
  7.2 0.0 copy-start.4
  7.2 0.0 copy-start.2
  7.3 53.8 %shard_map.140 = (bf16[5,2240,128]{2,1,0:T(8,128)(2,1)}, bf16[5,2240,128]{2,1,0:T(8,128)(2,1)}, f32[7,32,320]{2,1,0:T(8,128)}, bf16[7,32,320]{2,1,0:T(8,128)(2,1)}) custom-call(bf16[2240,128]{1,0:T(8,128)(2,1)} %bitcast.23, bf16[2240,128]{1,0:T(8,128)(2,1)} %bitcast.25, bf16[2240,384]{1,0:T(8,128)(2,1)} %bitcast.29, bf16[2240,384]{1,0:T(8,128)(2,1)} %bitcast.30), custom_call_target="tpu_custom_call" | custom-call | tf_op jit(solution)/shard_map/pallas_call | solution.py:277
  61.1 0.0 copy-start.3
  61.1 0.0 all-gather.3.cloned.1.call-update
  61.1 0.0 copy-done
  61.1 0.6 gather_fusion
  61.8 0.0 copy-done.1
  61.8 0.6 gather_fusion.1
  62.4 0.0 copy-done.4
  62.4 0.1 copy.27
  62.5 0.6 gather_fusion.2
  63.1 0.1 broadcast_compare_fusion
  63.2 0.1 copy.28
  63.3 0.1 copy.29
  63.4 0.1 select_reduce_fusion
  63.5 0.6 reshape.46.list_ref
  64.1 0.0 copy-done.2
  64.1 0.6 gather_fusion.3
  64.8 0.0 copy-done.3
  64.8 1.5 %broadcast_in_dim.44.gain_ref = f32[2240,1]{1,0:T(8,128)} reshape(f32[2240]{0:T(1024)S(1)} %copy-done.3) | data formatting | bytes 17920 | tf_op jit(solution)/shard_map/broadcast_in_dim | solution.py:67
  66.3 0.5 convert_reduce_fusion
  66.8 0.6 pad_add_fusion.count_ref
  67.4 45.9 %shard_map.142 = bf16[2240,384]{1,0:T(8,128)(2,1)} custom-call(s32[3]{0:T(128)} %get-tuple-element.11.seen_ref, s32[18]{0:T(128)} %reshape.46.list_ref, s32[7]{0:T(128)} %pad_add_fusion.count_ref, bf16[2240,384]{1,0:T(8,128)(2,1)} %bitcast.27, bf16[2240,128]{1,0:T(8,128)(2,1)} %bitcast.33, bf16[2240,128]{1,0:T(8,128)(2,1)} %bitcast.34, ...), custom_call_target="tpu_custom_call" | custom-call | tf_op jit(solution)/shard_map/pallas_call | solution.py:152
  113.4 0.0 all-gather.3.cloned.1.call-done
  113.4 3.2 %fusion.prior_ref = f32[7,32,320]{2,1,0:T(8,128)} fusion(bf16[16,7,32,320]{3,2,1,0:T(8,128)(2,1)} %bitcast.22, pred[16]{0:T(512)(128)(4,1)S(1)} %iota_compare_fusion.1), kind=kLoop, calls=%fused_computation.5 | loop fusion | flops 3368960 | bytes 2580496 | tf_op jit(solution)/shard_map/reduce_sum | solution.py:321
  116.6 5.1 %shard_map.141 = bf16[2240,384]{1,0:T(8,128)(2,1)} custom-call(bf16[2240,384]{1,0:T(8,128)(2,1)} %bitcast.31, f32[7,32,320]{2,1,0:T(8,128)} %get-tuple-element.6.own_ref, f32[7,32,320]{2,1,0:T(8,128)} %fusion.prior_ref, f32[2240,1]{1,0:T(8,128)} %broadcast_in_dim.44.gain_ref), custom_call_target="tpu_custom_call" | custom-call | tf_op jit(solution)/shard_map/pallas_call | solution.py:62
  (9 shorter events, 0.1 us)
Async XLA Ops:
  7.2 54.0 %copy-start = (s32[16]{0:T(128)S(1)}, s32[16]{0:T(128)}, u32[]{:S(2)}) copy-start(s32[16]{0:T(128)} %param.21) | copy-start | bytes 196
  7.2 106.2 %all-gather.3.cloned.1.call-start = ((), (), s32[]{:S(2)}) async-start(), calls=%async_computation | async-start | bytes 2924544 | tf_op jit(solution)/shard_map/all_gather | solution.py:319
  7.2 54.6 %copy-start.1 = (s32[16]{0:T(128)S(1)}, s32[16]{0:T(128)}, u32[]{:S(2)}) copy-start(s32[16]{0:T(128)} %param.22) | copy-start | bytes 196
  7.2 55.2 %copy-start.4 = (s32[16,3]{0,1:T(4,128)S(1)}, s32[16,3]{0,1:T(4,128)}, u32[]{:S(2)}) copy-start(s32[16,3]{0,1:T(4,128)} %param.24) | copy-start | bytes 580
  7.2 56.9 %copy-start.2 = (s32[16]{0:T(128)S(1)}, s32[16]{0:T(128)}, u32[]{:S(2)}) copy-start(s32[16]{0:T(128)} %param.23) | copy-start | bytes 196
  61.1 3.7 %copy-start.3 = (f32[2240]{0:T(1024)S(1)}, f32[2240]{0:T(1024)}, u32[]{:S(2)}) copy-start(f32[2240]{0:T(1024)} %param.25) | copy-start | bytes 26884
Sparse Core Ops, SparseCore 0:
  61.2 42.6 all-gather.2
